TPU v7x, 128 devices: a whole 4x4x4 slice. The times are simulated.
128 devices in a mesh: cells: 128 (over z, y, x, core).
Axes of the slice: x: 4, y: 4, z: 4, core: 2. Of those that a mesh axis runs over, the one named last changes fastest.
Arguments:
- ll_fields: bfloat16 [8, 2097152], P(None, 'cells'), may hold values from -6 to 6
- target: bfloat16 [8, 2097152], P(None, 'cells'), may hold values from -6 to 6
- in_rows: int32 [128, 128, 512], P('cells'), may hold values from 0 to 16383, as said below
- in_slot: int32 [4, 524288], P(None, 'cells'), may hold values from 0 to 65535, as said below
- in_weight: float32 [4, 524288], P(None, 'cells'), may hold values from 0.1 to 0.6
- neighbours: int32 [9, 524288], P(None, 'cells'), may hold values from 0 to 4643, as said below
- conv_weight: bfloat16 [64, 72], replicated, may hold values from -0.75 to 0.75
- up_weight: bfloat16 [256, 64], replicated, may hold values from -0.75 to 0.75
- down_weight: bfloat16 [64, 256], replicated, may hold values from -0.375 to 0.375
- head_weight: bfloat16 [8, 64], replicated, may hold values from -0.75 to 0.75
- out_rows: int32 [128, 128, 512], P('cells'), may hold values from 0 to 4095, as said below
- out_slot: int32 [4, 2097152], P(None, 'cells'), may hold values from 0 to 65535, as said below
- out_weight: float32 [4, 2097152], P(None, 'cells'), may hold values from 0.1 to 0.6
Outputs:
- predicted: bfloat16 [8, 2097152], P(None, 'cells')
- grad_conv: float32 [64, 72], replicated
- grad_up: float32 [256, 64], replicated
- grad_down: float32 [64, 256], replicated
- grad_head: float32 [8, 64], replicated
Inputs may be any that keep to these rules, and one draw needn't show every extreme that they name: `in_rows`: local point indices of the sending band. `in_slot`: entry (t, c) is b * 512 + s, a slot received from band b; for each band and tile only the first slots up to a count of 1 to 512 are read, and some slots are read by no cell. `out_rows`: local cell indices of the sending tile. `out_slot`: entry (t, p) is d * 512 + s, a slot received from tile d; for each tile and band only the first slots up to a count of 1 to 512 are read. `neighbours`: positions in the cell's tile bordered by one cell on every side, 18 rows of 258, row major. Entry k names the cell at row offset k // 3 - 1 and column offset k % 3 - 1 from the cell, except at the four corner cells of a tile, where the outward diagonal entry may name the edge neighbour one row away in the same column.
All inputs are finite; a program needn't handle non-finite values.
Results may differ from a plain program's by a relative error of at most 0.0048.
The roundings to bfloat16 on the way count: a program that leaves them out, or rounds other values in their place, can miss the bound.
Values may be sent and summed in bfloat16 or wider, within the bound.
No kernel may reach another device: no remote copies, remote signals or barrier semaphores. Data moves between devices by JAX's collectives and lax.ppermute only.
A program may use at most 192 MiB of HBM per device.

v0:
```python
import math

import jax
import jax.numpy as jnp
from jax import lax
from jax.sharding import PartitionSpec as P

VARS = 8
GRID_ROWS = 8
TILE_ROWS = 16
TILE_WIDTH = 256


def from_behind(value, axis, by):
    devices = lax.axis_size(axis)
    return lax.ppermute(value, axis, [(i, (i + by) % devices) for i in range(devices)])


def spread_taps(flattened, slot_table, weight_table):
    running = jnp.zeros((flattened.shape[0], slot_table.shape[1]), jnp.float32)
    for tap_index in range(slot_table.shape[0]):
        running = running + weight_table[tap_index] * flattened[:, slot_table[tap_index]].astype(
            jnp.float32
        )
    return running


def outer_sum(first_side, second_side):
    return lax.dot_general(
        first_side, second_side, (((1,), (1,)), ((), ())), preferred_element_type=jnp.float32
    )


def stencil_stack(padded, neighbours):
    row_count = padded.shape[1] - 2
    col_count = padded.shape[2] - 2
    pieces = [
        padded[
            :,
            direction // 3 : direction // 3 + row_count,
            direction % 3 : direction % 3 + col_count,
        ].reshape(padded.shape[0], row_count * col_count)
        for direction in range(9)
    ]
    stacked = jnp.stack(pieces, axis=1)
    corner_cells = jnp.array(
        [0, col_count - 1, (row_count - 1) * col_count, row_count * col_count - 1], jnp.int32
    )
    flat_padded = padded.reshape(padded.shape[0], -1)
    corner_values = flat_padded[:, neighbours[:, corner_cells]]
    stacked = stacked.at[:, :, corner_cells].set(corner_values)
    return stacked.reshape(-1, row_count * col_count)


def tile_forward(stacked, conv_weight, up_weight, down_weight, head_weight):
    conv_out = jnp.dot(conv_weight, stacked, preferred_element_type=jnp.float32)
    conv_bf = conv_out.astype(jnp.bfloat16)
    pre_act = jnp.dot(up_weight, conv_bf, preferred_element_type=jnp.float32)
    activated = jax.nn.gelu(pre_act).astype(jnp.bfloat16)
    mixed_bf = (
        conv_out + jnp.dot(down_weight, activated, preferred_element_type=jnp.float32)
    ).astype(jnp.bfloat16)
    head_out = jnp.dot(head_weight, mixed_bf, preferred_element_type=jnp.float32).astype(
        jnp.bfloat16
    )
    return (stacked, conv_bf, pre_act, activated, mixed_bf, head_out)


def tile_backward(saved, grad_out, up_weight, down_weight, head_weight):
    stacked, conv_bf, pre_act, activated, mixed_bf, head_out = saved
    grad_mixed = jnp.dot(head_weight.T, grad_out, preferred_element_type=jnp.float32)
    grad_mixed_bf = grad_mixed.astype(jnp.bfloat16)
    grad_head = outer_sum(grad_out, mixed_bf)
    grad_act = jnp.dot(down_weight.T, grad_mixed_bf, preferred_element_type=jnp.float32)
    grad_pre = jax.vjp(jax.nn.gelu, pre_act)[1](grad_act)[0].astype(jnp.bfloat16)
    grad_down = outer_sum(grad_mixed_bf, activated)
    grad_up = outer_sum(grad_pre, conv_bf)
    grad_conv_out = (
        grad_mixed + jnp.dot(up_weight.T, grad_pre, preferred_element_type=jnp.float32)
    ).astype(jnp.bfloat16)
    grad_conv = outer_sum(grad_conv_out, stacked)
    return (grad_conv, grad_up, grad_down, grad_head)


def column_from(piece_part, offset):
    return from_behind(piece_part, "cells", offset)


def row_from(piece_part, offset):
    return from_behind(piece_part, "cells", offset)


def body(
    ll_fields,
    target,
    in_rows,
    in_slot,
    in_weight,
    neighbours,
    conv_weight,
    up_weight,
    down_weight,
    head_weight,
    out_rows,
    out_slot,
    out_weight,
):
    devices = lax.axis_size("cells")
    tile_cols = devices // GRID_ROWS
    outgoing = ll_fields[:, in_rows[0]]
    received = lax.all_to_all(outgoing, "cells", split_axis=1, concat_axis=1, tiled=True)
    regridded = spread_taps(received.reshape(VARS, -1), in_slot, in_weight).astype(jnp.bfloat16)
    regridded = regridded.reshape(VARS, TILE_ROWS, TILE_WIDTH)
    left_col = column_from(regridded[:, :, TILE_WIDTH - 1], 1)
    right_col = column_from(regridded[:, :, 0], -1)
    middle = jnp.concatenate([left_col[:, :, None], regridded, right_col[:, :, None]], axis=2)
    upper_line = row_from(middle[:, TILE_ROWS - 1, :], tile_cols)
    lower_line = row_from(middle[:, 0, :], -tile_cols)
    padded = jnp.concatenate([upper_line[:, None, :], middle, lower_line[:, None, :]], axis=1)
    stacked = stencil_stack(padded, neighbours)
    saved = tile_forward(stacked, conv_weight, up_weight, down_weight, head_weight)
    head_out = saved[5]
    sending = head_out[:, out_rows[0]]
    arrived = lax.all_to_all(sending, "cells", split_axis=1, concat_axis=1, tiled=True)
    arrived = arrived.reshape(VARS, -1)
    predicted = spread_taps(arrived, out_slot, out_weight).astype(jnp.bfloat16)
    loss_scale = 1.0 / math.sqrt(ll_fields.shape[1] * devices)
    grad_pred = (predicted.astype(jnp.float32) - target.astype(jnp.float32)) * loss_scale
    slot_grad = jnp.zeros(arrived.shape, jnp.float32)
    for tap_index in range(out_slot.shape[0]):
        slot_grad = slot_grad.at[:, out_slot[tap_index]].add(out_weight[tap_index] * grad_pred)
    slot_grad = slot_grad.astype(jnp.bfloat16).reshape(VARS, devices, -1)
    returned = lax.all_to_all(slot_grad, "cells", split_axis=1, concat_axis=1, tiled=True)
    grad_out = jnp.zeros((VARS, head_out.shape[1]), jnp.float32)
    grad_out = grad_out.at[:, out_rows[0].reshape(-1)].add(
        returned.reshape(VARS, -1).astype(jnp.float32)
    )
    terms = tile_backward(saved, grad_out.astype(jnp.bfloat16), up_weight, down_weight, head_weight)
    totals = lax.psum((terms[0], terms[1], terms[2], terms[3]), "cells")
    return (predicted, totals[0], totals[1], totals[2], totals[3])


def solution(mesh):
    placed = (
        P(None, "cells"),
        P(None, "cells"),
        P("cells", None, None),
        P(None, "cells"),
        P(None, "cells"),
        P(None, "cells"),
        P(),
        P(),
        P(),
        P(),
        P("cells", None, None),
        P(None, "cells"),
        P(None, "cells"),
    )
    return jax.shard_map(
        body,
        mesh=mesh,
        in_specs=placed,
        out_specs=(P(None, "cells"), P(), P(), P(), P()),
        check_vma=False,
    )
```

profile of v0, /device:TPU:1, one launch (start us, length us, event | category | flops | bytes accessed | tf_op | source)
XLA Modules:
  0.0 1987.4 jit_solution(2743976166158285373)
XLA Ops:
  11.4 222.2 %gather_fusion = bf16[65536,8]{1,0:T(8,128)(2,1)} fusion(bf16[8,16384]{0,1:T(8,128)(2,1)} %copy.258, s32[65536]{0:T(1024)S(1)} %broadcast_clamp_fusion.1), kind=kCustom, calls=%fused_computation | custom fusion | bytes 2359296 | tf_op jit(solution)/shard_map/gather | solution.py:110
  233.6 12.6 copy.259
  246.1 11.9 all-to-all-start
  277.9 10.7 copy.260
  288.6 19.0 gather_fusion.1
  309.0 22.3 %gather_fusion.2 = bf16[4096,8]{1,0:T(8,128)(2,1)} fusion(bf16[8,65536]{0,1:T(8,128)(2,1)} %bitcast.158, s32[4096]{0:T(1024)S(1)} %copy-done.33), kind=kCustom, calls=%fused_computation.2 | custom fusion | bytes 147456 | tf_op jit(solution)/shard_map/gather | solution.py:22
  333.8 22.8 %gather_fusion.3 = bf16[4096,8]{1,0:T(8,128)(2,1)} fusion(bf16[8,65536]{0,1:T(8,128)(2,1)} %bitcast.159, s32[4096]{0:T(1024)S(1)} %copy-done.32), kind=kCustom, calls=%fused_computation.3 | custom fusion | bytes 147456 | tf_op jit(solution)/shard_map/gather | solution.py:22
  359.2 23.6 %gather_fusion.4 = bf16[4096,8]{1,0:T(8,128)(2,1)} fusion(bf16[8,65536]{0,1:T(8,128)(2,1)} %bitcast.160, s32[4096]{0:T(1024)} %get-tuple-element.79), kind=kCustom, calls=%fused_computation.4 | custom fusion | bytes 147456 | tf_op jit(solution)/shard_map/gather | solution.py:22
  388.4 5.4 fusion.12
  403.3 7.6 copy.277
  412.8 9.3 reshape.699
  426.0 229.0 %gather_fusion.7 = bf16[65536,8]{1,0:T(8,128)(2,1)} fusion(bf16[8,4096]{0,1:T(8,128)(2,1)S(1)} %copy.280, s32[65536]{0:T(1024)S(1)} %broadcast_clamp_fusion), kind=kCustom, calls=%fused_computation.7 | custom fusion | bytes 2359296 | tf_op jit(solution)/shard_map/gather | solution.py:123
  655.0 12.6 copy.281
  667.6 13.9 all-to-all-start.1
  683.9 16.8 all-to-all-done.1
  700.6 10.7 copy.282
  711.4 63.3 %gather_fusion.8 = bf16[16384,8]{1,0:T(8,128)(2,1)} fusion(bf16[8,65536]{0,1:T(8,128)(2,1)} %bitcast.153, s32[16384]{0:T(1024)S(1)} %copy-done.22), kind=kCustom, calls=%fused_computation.8 | custom fusion | bytes 589824 | tf_op jit(solution)/shard_map/gather | solution.py:22
  778.4 63.3 %gather_fusion.9 = bf16[16384,8]{1,0:T(8,128)(2,1)} fusion(bf16[8,65536]{0,1:T(8,128)(2,1)} %bitcast.154, s32[16384]{0:T(1024)S(1)} %copy-done.21), kind=kCustom, calls=%fused_computation.9 | custom fusion | bytes 589824 | tf_op jit(solution)/shard_map/gather | solution.py:22
  845.4 63.3 %gather_fusion.10 = bf16[16384,8]{1,0:T(8,128)(2,1)} fusion(bf16[8,65536]{0,1:T(8,128)(2,1)} %bitcast.155, s32[16384]{0:T(1024)S(1)} %copy-done.24), kind=kCustom, calls=%fused_computation.10 | custom fusion | bytes 589824 | tf_op jit(solution)/shard_map/gather | solution.py:22
  912.5 63.3 %gather_fusion.11 = bf16[16384,8]{1,0:T(8,128)(2,1)} fusion(bf16[8,65536]{0,1:T(8,128)(2,1)} %bitcast.156, s32[16384]{0:T(1024)S(1)} %copy-done.23), kind=kCustom, calls=%fused_computation.11 | custom fusion | bytes 589824 | tf_op jit(solution)/shard_map/gather | solution.py:22
  996.8 5.2 copy.290
  1002.0 100.8 %scatter_custom_fusion.1 = f32[8,65536]{0,1:T(8,128)} fusion(s32[16384]{0:T(1024)} %bitcast.194, f32[16384,8]{1,0:T(8,128)} %copy.287, f32[]{:T(128)} %constant.3.clone.1), kind=kCustom, calls=%fused_computation.18 | custom fusion | flops 131072 | bytes 2097664 | tf_op jit(solution)/shard_map/scatter-add | solution.py:131
  1102.7 100.4 %scatter_fusion.1 = f32[8,65536]{0,1:T(8,128)} fusion(f32[8,65536]{0,1:T(8,128)} %scatter_custom_fusion.1, s32[16384]{0:T(1024)S(1)} %bitcast.177, f32[16384,8]{1,0:T(8,128)} %copy.288), kind=kCustom, calls=%fused_computation.14 | custom fusion | flops 131072 | bytes 1638400 | tf_op jit(solution)/shard_map/scatter-add | solution.py:131
  1203.1 100.7 %scatter_fusion.2 = f32[8,65536]{0,1:T(8,128)} fusion(f32[8,65536]{0,1:T(8,128)} %scatter_fusion.1, s32[16384]{0:T(1024)S(1)} %bitcast.175, f32[16384,8]{1,0:T(8,128)} %copy.289), kind=kCustom, calls=%fused_computation.15 | custom fusion | flops 131072 | bytes 1638400 | tf_op jit(solution)/shard_map/scatter-add | solution.py:131
  1303.8 100.3 %scatter_fusion.3 = f32[8,65536]{0,1:T(8,128)} fusion(f32[8,65536]{0,1:T(8,128)} %scatter_fusion.2, s32[16384]{0:T(1024)S(1)} %bitcast.173, f32[16384,8]{1,0:T(8,128)} %copy.290), kind=kCustom, calls=%fused_computation.16 | custom fusion | flops 131072 | bytes 1638400 | tf_op jit(solution)/shard_map/scatter-add | solution.py:131
  1404.1 17.1 convert_element_type.180
  1421.3 12.6 copy.291
  1438.6 19.0 all-to-all-done.2
  1460.0 16.7 copy.292
  1476.6 348.0 %scatter_custom_fusion.5 = f32[8,4096]{0,1:T(8,128)S(1)} fusion(s32[65536]{0:T(1024)S(1)} %bitcast.192, f32[65536,8]{1,0:T(8,128)} %copy.292, f32[]{:T(128)} %constant.3.clone.1), kind=kCustom, calls=%fused_computation.48 | custom fusion | flops 524288 | bytes 131584 | tf_op jit(solution)/shard_map/scatter-add | solution.py:135
  1839.3 63.3 %all-reduce = (f32[64,72]{1,0:T(8,128)}, f32[8,64]{1,0:T(8,128)}) all-reduce(f32[64,72]{1,0:T(8,128)S(1)} %fusion.15, f32[8,64]{1,0:T(8,128)S(1)} %fusion.18), channel_id=1, replica_groups=mesh['cells'=128] {'cells'}, use_global_device_ids=true, to_apply=%region_6.0 | all-reduce | flops 5120 | bytes 40960 | tf_op jit(solution)/shard_map/psum | solution.py:139
  1902.6 74.9 %all-reduce.4.cloned.1.call-done = (f32[256,64]{0,1:T(8,128)}, f32[64,256]{1,0:T(8,128)}) async-done(((f32[256,64]{0,1:T(8,128)}, f32[64,256]{1,0:T(8,128)}), (f32[256,64]{0,1:T(8,128)}, f32[64,256]{1,0:T(8,128)})) %all-reduce.4.cloned.1.call-update) | async-done | bytes 131088 | tf_op jit(solution)/shard_map/psum | solution.py:139
  (188 shorter events, 110.2 us)
Async XLA Ops:
  7.2 416.2 %copy-start = (bf16[64,256]{1,0:T(8,128)(2,1)S(1)}, bf16[64,256]{1,0:T(8,128)(2,1)}, u32[]{:S(2)}) copy-start(bf16[64,256]{1,0:T(8,128)(2,1)} %param.22) | copy-start | bytes 98308
  233.5 24.5 %copy-start.31 = (s32[4,4096]{1,0:T(4,128)S(1)}, s32[4,4096]{1,0:T(4,128)}, u32[]{:S(2)}) copy-start(s32[4,4096]{1,0:T(4,128)} %param.17) | copy-start | bytes 196612
  233.5 25.2 %copy-start.28 = (f32[4,4096]{1,0:T(4,128)S(1)}, f32[4,4096]{1,0:T(4,128)}, u32[]{:S(2)}) copy-start(f32[4,4096]{1,0:T(4,128)} %param.18) | copy-start | bytes 196612
  246.1 15.5 copy-start.38
  246.1 16.1 copy-start.11
  246.1 31.7 %all-to-all-start = ((bf16[8,128,512]{2,0,1:T(8,128)(2,1)}), bf16[8,128,512]{2,0,1:T(8,128)(2,1)S(1)}, u32[]{:S(2)}, u32[]{:S(2)}) async-start(bf16[8,128,512]{2,0,1:T(8,128)(2,1)} %bitcast.3), calls=%async_computation | async-start | bytes 2097152 | tf_op jit(solution)/shard_map/all_to_all | solution.py:111
  288.6 20.4 %copy-start.33 = (s32[4096]{0:T(1024)S(1)}, s32[4096]{0:T(1024)}, u32[]{:S(2)}) copy-start(s32[4096]{0:T(1024)} %get-tuple-element.81) | copy-start | bytes 49156
  307.7 26.1 %copy-start.32 = (s32[4096]{0:T(1024)S(1)}, s32[4096]{0:T(1024)}, u32[]{:S(2)}) copy-start(s32[4096]{0:T(1024)} %get-tuple-element.80) | copy-start | bytes 49156
  358.0 27.4 %copy-start.29 = (f32[16,256]{1,0:T(8,128)S(1)}, f32[16,256]{1,0:T(8,128)}, u32[]{:S(2)}) copy-start(f32[16,256]{1,0:T(8,128)} %mul.224) | copy-start | bytes 49156
  358.0 27.4 %copy-start.30 = (f32[16,256]{1,0:T(8,128)S(1)}, f32[16,256]{1,0:T(8,128)}, u32[]{:S(2)}) copy-start(f32[16,256]{1,0:T(8,128)} %mul.227) | copy-start | bytes 49156
  386.7 7.4 collective-permute-start
  388.4 5.9 collective-permute-start.1
  388.4 13.9 copy-start.35
  394.6 6.7 collective-permute-start.2
  397.4 4.0 collective-permute-start.3
  425.3 229.7 %copy-start.7 = (bf16[4096,64]{0,1:T(8,128)(2,1)}, bf16[4096,64]{0,1:T(8,128)(2,1)S(1)}, u32[]{:S(2)}) copy-start(bf16[4096,64]{0,1:T(8,128)(2,1)S(1)} %fusion.2) | copy-start | bytes 1572868
  655.0 26.5 %copy-start.18 = (f32[1,16384]{1,0:T(1,128)S(1)}, f32[1,16384]{1,0:T(1,128)}, u32[]{:S(2)}) copy-start(f32[1,16384]{1,0:T(1,128)} %get-tuple-element.52) | copy-start | bytes 196612
  655.0 26.6 %copy-start.12 = (s32[1,128,512]{2,1,0:T(8,128)S(1)}, s32[1,128,512]{2,1,0:T(8,128)}, u32[]{:S(2)}) copy-start(s32[1,128,512]{2,1,0:T(8,128)} %param.24) | copy-start | bytes 786436
  655.0 27.6 %copy-start.17 = (f32[1,16384]{1,0:T(1,128)S(1)}, f32[1,16384]{1,0:T(1,128)}, u32[]{:S(2)}) copy-start(f32[1,16384]{1,0:T(1,128)} %get-tuple-element.50) | copy-start | bytes 196612
  655.0 28.2 %copy-start.19 = (f32[1,16384]{1,0:T(1,128)S(1)}, f32[1,16384]{1,0:T(1,128)}, u32[]{:S(2)}) copy-start(f32[1,16384]{1,0:T(1,128)} %get-tuple-element.51) | copy-start | bytes 196612
  655.0 28.2 %copy-start.20 = (f32[1,16384]{1,0:T(1,128)S(1)}, f32[1,16384]{1,0:T(1,128)}, u32[]{:S(2)}) copy-start(f32[1,16384]{1,0:T(1,128)} %get-tuple-element.53) | copy-start | bytes 196612
  667.6 33.0 %all-to-all-start.1 = ((bf16[8,128,512]{2,0,1:T(8,128)(2,1)}), bf16[8,128,512]{2,0,1:T(8,128)(2,1)S(1)}, u32[]{:S(2)}, u32[]{:S(2)}) async-start(bf16[8,128,512]{2,0,1:T(8,128)(2,1)} %bitcast.47), calls=%async_computation.1 | async-start | bytes 2097152 | tf_op jit(solution)/shard_map/all_to_all | solution.py:124
  683.9 27.5 %copy-start.22 = (s32[16384]{0:T(1024)S(1)}, s32[16384]{0:T(1024)}, u32[]{:S(2)}) copy-start(s32[16384]{0:T(1024)} %broadcast_clamp_fusion.5) | copy-start | bytes 196612
  711.4 67.0 %copy-start.21 = (s32[16384]{0:T(1024)S(1)}, s32[16384]{0:T(1024)}, u32[]{:S(2)}) copy-start(s32[16384]{0:T(1024)} %broadcast_clamp_fusion.4) | copy-start | bytes 196612
  778.4 67.0 %copy-start.24 = (s32[16384]{0:T(1024)S(1)}, s32[16384]{0:T(1024)}, u32[]{:S(2)}) copy-start(s32[16384]{0:T(1024)} %broadcast_clamp_fusion.3) | copy-start | bytes 196612
  845.4 67.0 %copy-start.23 = (s32[16384]{0:T(1024)S(1)}, s32[16384]{0:T(1024)}, u32[]{:S(2)}) copy-start(s32[16384]{0:T(1024)} %broadcast_clamp_fusion.2) | copy-start | bytes 196612
  912.5 67.2 %copy-start.9 = (bf16[8,16384]{1,0:T(8,128)(2,1)S(1)}, bf16[8,16384]{1,0:T(8,128)(2,1)}, u32[]{:S(2)}) copy-start(bf16[8,16384]{1,0:T(8,128)(2,1)} %param.15) | copy-start | bytes 786436
  1002.0 100.8 %copy-start.16 = (s32[16384,1]{0,1:T(1,128)S(1)}, s32[16384,1]{0,1:T(1,128)}, u32[]{:S(2)}) copy-start(s32[16384,1]{0,1:T(1,128)} %copy-done.15) | copy-start | bytes 196612
  1102.7 100.4 %copy-start.14 = (s32[16384,1]{0,1:T(1,128)S(1)}, s32[16384,1]{0,1:T(1,128)}, u32[]{:S(2)}) copy-start(s32[16384,1]{0,1:T(1,128)} %get-tuple-element.57) | copy-start | bytes 196612
  1421.3 17.0 copy-start.13
  1433.8 23.8 %all-to-all-start.2 = ((bf16[8,128,512]{2,0,1:T(8,128)(2,1)}), bf16[8,128,512]{2,0,1:T(8,128)(2,1)S(1)}, u32[]{:S(2)}, u32[]{:S(2)}) async-start(bf16[8,128,512]{2,0,1:T(8,128)(2,1)} %copy.291), calls=%async_computation.2 | async-start | bytes 2097152 | tf_op jit(solution)/shard_map/all_to_all | solution.py:133
  1438.2 539.2 %all-reduce.4.cloned.1.call-start = ((), (), s32[]{:S(2)}) async-start(), calls=%async_computation.3 | async-start | bytes 262144 | tf_op jit(solution)/shard_map/psum | solution.py:139
  (16 other events, 66.3 us)
Sparse Core Ops, SparseCore 0:
  1839.0 138.4 all-reduce.3
where the time goes:
time: 1990 us
  local copies, waits for them, and re-layouts  951 us (48%)
  other arithmetic  793 us (40%)
  waiting for transfers between devices  111 us (6%)
  blocking collectives  63.3 us (3%)
  starting transfers between devices  37.7 us (2%)
    scatter-add x4, other arithmetic, body(): slot_grad.at[:, out_slot[tap_index]].add(out_weight[tap_index] * grad_pred)  402 us
    gather x12, local copies, waits for them, and re-layouts, spread_taps(): flattened[:, slot_table[tap_index]].astype(jnp.float32)  356 us
    scatter-add x1, other arithmetic, body(): grad_out.at[:, out_rows[0].reshape(-1)]  348 us
    gather x2, local copies, waits for them, and re-layouts, body(): sending = head_out[:, out_rows[0]]  242 us
    gather x2, local copies, waits for them, and re-layouts, body(): outgoing = ll_fields[:, in_rows[0]]  235 us
    psum x1, waiting for transfers between devices, body(): totals = lax.psum((terms[0], terms[1], terms[2], terms[3]), 'cells')  74.9 us
    psum x1, blocking collectives, body(): totals = lax.psum((terms[0], terms[1], terms[2], terms[3]), 'cells')  63.3 us
  transfers between devices with their start and end apart: 8, of which 4 were waited for; matrix products, arithmetic and copies ran while one was open for 1% of the time, Pallas kernels for 0%

commit v1 on v0

--- a/solution.py
+++ b/solution.py
@@ -1,28 +1,179 @@
-import math
-
-import jax
-import jax.numpy as jnp
+import functools, math
+import jax, jax.numpy as jnp
 from jax import lax
 from jax.sharding import PartitionSpec as P
+from jax.experimental import pallas as pl
+from jax.experimental.pallas import tpu as pltpu
+BF=jnp.bfloat16; F32=jnp.float32; I16=jnp.int16; I32=jnp.int32
+
+def onehot(h, n):
+    it = lax.broadcasted_iota(I16, (n, h.shape[1]), 0)
+    hh = jnp.broadcast_to(h.astype(I16), (n, h.shape[1]))
+    return jnp.where(it == hh, jnp.ones((), BF), jnp.zeros((), BF))
+
+def pick(mm, lo, base, count, acc):
+    l8 = jnp.broadcast_to(lo, (8, lo.shape[1]))
+    for k in range(count):
+        acc = jnp.where(l8 == base + k, mm[8*k:8*k+8], acc)
+    return acc
+
+def k4_body(BP, tab_ref, tgt_ref, slot_ref, w_ref, pred_ref, send_ref, oh_ref, e_ref, acc_ref):
+    i = pl.program_id(0)
+    scale = 1.0 / math.sqrt(2097152)
+    def tap(t, p):
+        idx = slot_ref[pl.ds(t,1), :]
+        oh = onehot(idx & 511, 512)
+        oh_ref[t] = oh
+        d = idx >> 9
+        def rows(r, a):
+            mm = jnp.dot(tab_ref[pl.ds(pl.multiple_of(r*256,256), 256), :], oh, preferred_element_type=F32)
+            return pick(mm, d - r*32, 0, 32, a)
+        a = lax.fori_loop(0, 4, rows, jnp.zeros((8, BP), F32))
+        return p + w_ref[pl.ds(t,1), :] * a
+    p = lax.fori_loop(0, 4, tap, jnp.zeros((8, BP), F32))
+    pb = p.astype(BF)
+    pred_ref[...] = pb
+    g = (pb.astype(F32) - tgt_ref[...].astype(F32)) * scale
+    @pl.when(i == 0)
+    def _(): acc_ref[...] = jnp.zeros_like(acc_ref)
+    half = lax.broadcasted_iota(I16, (16, BP), 0) >> 3
+    def back(t, c):
+        idx = slot_ref[pl.ds(t,1), :]
+        d = idx >> 9
+        val = (w_ref[pl.ds(t,1), :] * g).astype(BF)
+        val2 = jnp.concatenate([val, val], axis=0)
+        q = jnp.broadcast_to(d.astype(I16), (16, BP)) - half
+        z = jnp.zeros((), BF)
+        for k in range(64):
+            e_ref[16*k:16*k+16, :] = jnp.where(q == jnp.int16(2*k), val2, z)
+        acc_ref[...] += lax.dot_general(e_ref[...], oh_ref[t], (((1,), (1,)), ((), ())), preferred_element_type=F32)
+        return c
+    lax.fori_loop(0, 4, back, 0)
+    @pl.when(i == pl.num_programs(0)-1)
+    def _(): send_ref[...] = acc_ref[...].astype(BF)
+
+def k4(tab, target, slot, w, BP=512):
+    points = target.shape[1]
+    return pl.pallas_call(
+        functools.partial(k4_body, BP),
+        grid=(points//BP,),
+        in_specs=[pl.BlockSpec((1024,512), lambda i:(0,0)), pl.BlockSpec((8,BP), lambda i:(0,i)),
+                  pl.BlockSpec((4,BP), lambda i:(0,i)), pl.BlockSpec((4,BP), lambda i:(0,i))],
+        out_specs=[pl.BlockSpec((8,BP), lambda i:(0,i)), pl.BlockSpec((1024,512), lambda i:(0,0))],
+        out_shape=[jax.ShapeDtypeStruct((8,points), BF), jax.ShapeDtypeStruct((1024,512), BF)],
+        scratch_shapes=[pltpu.VMEM((4,512,BP), BF), pltpu.VMEM((1024,BP), BF), pltpu.VMEM((1024,512), F32)],
+        name="k4",
+    )(tab, target, slot, w)
+
+def k1_body(ll_ref, rows_ref, out_ref, tab_ref):
+    @pl.when(pl.program_id(0) == 0)
+    def _():
+        for k in range(32):
+            a = ll_ref[:, 512*k:512*k+256]; b = ll_ref[:, 512*k+256:512*k+512]
+            tab_ref[16*k:16*k+16, :] = jnp.concatenate([a, b], axis=0)
+    def pair(j, c):
+        outs = []
+        for u in range(2):
+            idx = rows_ref[pl.ds(2*j+u, 1), :]
+            oh = onehot(idx & 255, 256)
+            lo = idx >> 8
+            def rr(r, a):
+                mm = jnp.dot(tab_ref[pl.ds(pl.multiple_of(r*256,256), 256), :], oh, preferred_element_type=F32)
+                return pick(mm, lo - r*32, 0, 32, a)
+            outs.append(lax.fori_loop(0, 2, rr, jnp.zeros((8, 512), F32)))
+        out_ref[pl.ds(pl.multiple_of(16*j,16),16), :] = jnp.concatenate(outs, 0).astype(BF)
+        return c
+    lax.fori_loop(0, 4, pair, 0)
+
+def k1(ll, rows):
+    return pl.pallas_call(k1_body, grid=(16,),
+        in_specs=[pl.BlockSpec((8,16384), lambda i:(0,0)), pl.BlockSpec((8,512), lambda i:(i,0))],
+        out_specs=pl.BlockSpec((64,512), lambda i:(i,0)),
+        out_shape=jax.ShapeDtypeStruct((1024,512), BF),
+        scratch_shapes=[pltpu.VMEM((512,256), BF)], name="k1")(ll, rows)
+
+def k2_body(tab_ref, slot_ref, w_ref, out_ref):
+    def tap(t, p):
+        idx = slot_ref[pl.ds(t,1), :]
+        oh = onehot(idx & 511, 512)
+        d = idx >> 9
+        def rows(r, a):
+            mm = jnp.dot(tab_ref[pl.ds(pl.multiple_of(r*256,256), 256), :], oh, preferred_element_type=F32)
+            return pick(mm, d - r*32, 0, 32, a)
+        a = lax.fori_loop(0, 4, rows, jnp.zeros((8, 512), F32))
+        return p + w_ref[pl.ds(t,1), :] * a
+    p = lax.fori_loop(0, 4, tap, jnp.zeros((8, 512), F32))
+    out_ref[...] = p.astype(BF)
+
+def k2(tab, slot, w):
+    return pl.pallas_call(k2_body, grid=(8,),
+        in_specs=[pl.BlockSpec((1024,512), lambda i:(0,0)), pl.BlockSpec((4,512), lambda i:(0,i)), pl.BlockSpec((4,512), lambda i:(0,i))],
+        out_specs=pl.BlockSpec((8,512), lambda i:(0,i)),
+        out_shape=jax.ShapeDtypeStruct((8,4096), BF), name="k2")(tab, slot, w)
+
+def k3_body(ho_ref, rows_ref, out_ref, tab_ref):
+    @pl.when(pl.program_id(0) == 0)
+    def _():
+        for k in range(8):
+            a = ho_ref[:, 512*k:512*k+256]; b = ho_ref[:, 512*k+256:512*k+512]
+            tab_ref[16*k:16*k+16, :] = jnp.concatenate([a, b], axis=0)
+    def pair(j, c):
+        outs = []
+        for u in range(2):
+            idx = rows_ref[pl.ds(2*j+u, 1), :]
+            oh = onehot(idx & 255, 256)
+            mm = jnp.dot(tab_ref[...], oh, preferred_element_type=F32)
+            outs.append(pick(mm, idx >> 8, 0, 16, jnp.zeros((8,512), F32)))
+        out_ref[pl.ds(pl.multiple_of(16*j,16),16), :] = jnp.concatenate(outs, 0).astype(BF)
+        return c
+    lax.fori_loop(0, 4, pair, 0)
+
+def k3(ho, rows):
+    return pl.pallas_call(k3_body, grid=(16,),
+        in_specs=[pl.BlockSpec((8,4096), lambda i:(0,0)), pl.BlockSpec((8,512), lambda i:(i,0))],
+        out_specs=pl.BlockSpec((64,512), lambda i:(i,0)),
+        out_shape=jax.ShapeDtypeStruct((1024,512), BF),
+        scratch_shapes=[pltpu.VMEM((128,256), BF)], name="k3")(ho, rows)
+
+def k5_body(sg_ref, rows_ref, out_ref, e_ref, oh_ref, acc_ref):
+    i = pl.program_id(0)
+    @pl.when(i == 0)
+    def _(): acc_ref[...] = jnp.zeros_like(acc_ref)
+    half = lax.broadcasted_iota(I16, (16, 512), 0) >> 3
+    z = jnp.zeros((), BF)
+    for j in range(4):
+        v2 = sg_ref[16*j:16*j+16, :]
+        for u in range(2):
+            val = v2[8*u:8*u+8]
+            val2 = jnp.concatenate([val, val], 0)
+            idx = rows_ref[2*j+u:2*j+u+1, :]
+            n0 = (2*j+u)*512
+            oh_ref[:, n0:n0+512] = onehot(idx & 255, 256)
+            q = jnp.broadcast_to((idx >> 8).astype(I16), (16, 512)) - half
+            for k in range(8):
+                e_ref[16*k:16*k+16, n0:n0+512] = jnp.where(q == jnp.int16(2*k), val2, z)
+    acc_ref[...] += lax.dot_general(e_ref[...], oh_ref[...], (((1,), (1,)), ((), ())), preferred_element_type=F32)
+    @pl.when(i == pl.num_programs(0)-1)
+    def _():
+        for k in range(16):
+            out_ref[:, 256*k:256*k+256] = acc_ref[8*k:8*k+8, :].astype(BF)
+
+def k5(sg, rows):
+    return pl.pallas_call(k5_body, grid=(16,),
+        in_specs=[pl.BlockSpec((64,512), lambda i:(i,0)), pl.BlockSpec((8,512), lambda i:(i,0))],
+        out_specs=pl.BlockSpec((8,4096), lambda i:(0,0)),
+        out_shape=jax.ShapeDtypeStruct((8,4096), BF),
+        scratch_shapes=[pltpu.VMEM((128,4096), BF), pltpu.VMEM((256,4096), BF), pltpu.VMEM((128,256), F32)], name="k5")(sg, rows)
+
 
 VARS = 8
 GRID_ROWS = 8
 TILE_ROWS = 16
 TILE_WIDTH = 256
 
-
 def from_behind(value, axis, by):
     devices = lax.axis_size(axis)
     return lax.ppermute(value, axis, [(i, (i + by) % devices) for i in range(devices)])
-
-
-def spread_taps(flattened, slot_table, weight_table):
-    running = jnp.zeros((flattened.shape[0], slot_table.shape[1]), jnp.float32)
-    for tap_index in range(slot_table.shape[0]):
-        running = running + weight_table[tap_index] * flattened[:, slot_table[tap_index]].astype(
-            jnp.float32
-        )
-    return running
 
 
 def outer_sum(first_side, second_side):
@@ -91,25 +242,16 @@
 
 
 def body(
-    ll_fields,
-    target,
-    in_rows,
-    in_slot,
-    in_weight,
-    neighbours,
-    conv_weight,
-    up_weight,
-    down_weight,
-    head_weight,
-    out_rows,
-    out_slot,
-    out_weight,
+    ll_fields, target, in_rows, in_slot, in_weight, neighbours, conv_weight, up_weight, down_weight,
+    head_weight, out_rows, out_slot, out_weight,
 ):
     devices = lax.axis_size("cells")
     tile_cols = devices // GRID_ROWS
-    outgoing = ll_fields[:, in_rows[0]]
-    received = lax.all_to_all(outgoing, "cells", split_axis=1, concat_axis=1, tiled=True)
-    regridded = spread_taps(received.reshape(VARS, -1), in_slot, in_weight).astype(jnp.bfloat16)
+    exchange = functools.partial(
+        lax.all_to_all, axis_name="cells", split_axis=0, concat_axis=0, tiled=True
+    )
+    received = exchange(k1(ll_fields, in_rows[0]))
+    regridded = k2(received, in_slot, in_weight)
     regridded = regridded.reshape(VARS, TILE_ROWS, TILE_WIDTH)
     left_col = column_from(regridded[:, :, TILE_WIDTH - 1], 1)
     right_col = column_from(regridded[:, :, 0], -1)
@@ -120,24 +262,19 @@
     stacked = stencil_stack(padded, neighbours)
     saved = tile_forward(stacked, conv_weight, up_weight, down_weight, head_weight)
     head_out = saved[5]
-    sending = head_out[:, out_rows[0]]
-    arrived = lax.all_to_all(sending, "cells", split_axis=1, concat_axis=1, tiled=True)
-    arrived = arrived.reshape(VARS, -1)
-    predicted = spread_taps(arrived, out_slot, out_weight).astype(jnp.bfloat16)
-    loss_scale = 1.0 / math.sqrt(ll_fields.shape[1] * devices)
-    grad_pred = (predicted.astype(jnp.float32) - target.astype(jnp.float32)) * loss_scale
-    slot_grad = jnp.zeros(arrived.shape, jnp.float32)
-    for tap_index in range(out_slot.shape[0]):
-        slot_grad = slot_grad.at[:, out_slot[tap_index]].add(out_weight[tap_index] * grad_pred)
-    slot_grad = slot_grad.astype(jnp.bfloat16).reshape(VARS, devices, -1)
-    returned = lax.all_to_all(slot_grad, "cells", split_axis=1, concat_axis=1, tiled=True)
-    grad_out = jnp.zeros((VARS, head_out.shape[1]), jnp.float32)
-    grad_out = grad_out.at[:, out_rows[0].reshape(-1)].add(
-        returned.reshape(VARS, -1).astype(jnp.float32)
-    )
-    terms = tile_backward(saved, grad_out.astype(jnp.bfloat16), up_weight, down_weight, head_weight)
-    totals = lax.psum((terms[0], terms[1], terms[2], terms[3]), "cells")
-    return (predicted, totals[0], totals[1], totals[2], totals[3])
+    arrived = exchange(k3(head_out, out_rows[0]))
+    predicted, slot_grad = k4(arrived, target, out_slot, out_weight)
+    returned = exchange(slot_grad)
+    grad_out = k5(returned, out_rows[0])
+    terms = tile_backward(saved, grad_out, up_weight, down_weight, head_weight)
+    flat = jnp.concatenate([term.reshape(-1) for term in terms]).reshape(devices, -1)
+    part = jnp.sum(exchange(flat), axis=0, keepdims=True)
+    whole = exchange(jnp.broadcast_to(part, flat.shape)).reshape(-1)
+    totals, at = [], 0
+    for term in terms:
+        totals.append(whole[at : at + term.size].reshape(term.shape))
+        at += term.size
+    return (predicted, *totals)
 
 
 def solution(mesh):

time: 1990 us -> 578 us (0.29)
  local copies, waits for them, and re-layouts: 951 us -> 30.4 us
  other arithmetic: 793 us -> 4.48 us
  Pallas kernels: 0 us -> 399 us
  waiting for transfers between devices: 111 us -> 21.1 us
  blocking collectives: 63.3 us -> 85.2 us
  starting transfers between devices: 37.7 us -> 16.2 us
    gather x16 -> x0, local copies, waits for them, and re-layouts: 832 us -> none  [the longest x12 356 us: spread_taps(): flattened[:, slot_table[tap_index]].astype(jnp.float32)]
    scatter-add x5 -> x0, other arithmetic: 750 us -> none  [the longest x4 402 us: body(): slot_grad.at[:, out_slot[tap_index]].add(out_weight[tap_index] * grad_pred)]
    pallas_call x0 -> x5, Pallas kernels: none -> 399 us  [the longest x1 262 us: k4(): pl.pallas_call(functools.partial(k4_body, BP), grid=(points // BP,), in_s...]
    all_to_all x0 -> x4, blocking collectives: none -> 85.2 us  [the longest x1 31.1 us: body(): arrived = exchange(k3(head_out, out_rows[0]))]
    psum x1 -> x0, waiting for transfers between devices: 74.9 us -> none  [body(): totals = lax.psum((terms[0], terms[1], terms[2], terms[3]), 'cells')]
    psum x1 -> x0, blocking collectives: 63.3 us -> none  [body(): totals = lax.psum((terms[0], terms[1], terms[2], terms[3]), 'cells')]
    mul x8 -> x0, local copies, waits for them, and re-layouts: 24.1 us -> none  [the longest x4 20.8 us: body(): out_weight[tap_index] * grad_pred]
    convert_element_type x7 -> x0, other arithmetic: 23.9 us -> none  [the longest x1 17.1 us: body(): slot_grad = slot_grad.astype(jnp.bfloat16).reshape(VARS, devices, -1)]
  transfers between devices with their start and end apart: 8 -> 5, of which waited for: 4 -> 5; matrix products, arithmetic and copies ran while one was open for 1% -> 1% of each run, Pallas kernels for 0% -> 0%
where the time goes in v1:
time: 578 us; the launch traced here: 576 us
  Pallas kernels  399 us (69%)
  blocking collectives  85.2 us (15%)
  local copies, waits for them, and re-layouts  30.4 us (5%)
  waiting for transfers between devices  21.1 us (4%)
  matrix products  18.6 us (3%)
  starting transfers between devices  16.2 us (3%)
    pallas_call x1, Pallas kernels, k4(): pl.pallas_call(functools.partial(k4_body, BP), grid=(points // BP,), in_s...  262 us
    pallas_call x1, Pallas kernels, k1(): pl.pallas_call(k1_body, grid=(16,), in_specs=[pl.BlockSpec((8, 16384), la...  62.8 us
    pallas_call x1, Pallas kernels, k2(): pl.pallas_call(k2_body, grid=(8,), in_specs=[pl.BlockSpec((1024, 512), la...  41.9 us
    all_to_all x1, blocking collectives, body(): arrived = exchange(k3(head_out, out_rows[0]))  31.1 us
    all_to_all x1, blocking collectives, body(): returned = exchange(slot_grad)  24.7 us
    pallas_call x1, Pallas kernels, k3(): pl.pallas_call(k3_body, grid=(16,), in_specs=[pl.BlockSpec((8, 4096), lam...  17.5 us
    all_to_all x1, waiting for transfers between devices, body(): received = exchange(k1(ll_fields, in_rows[0]))  16.9 us
    pallas_call x1, Pallas kernels, k5(): pl.pallas_call(k5_body, grid=(16,), in_specs=[pl.BlockSpec((64, 512), lam...  14.9 us
  transfers between devices with their start and end apart: 5, of which 5 were waited for; matrix products, arithmetic and copies ran while one was open for 1% of the time, Pallas kernels for 0%

profile of v1, /device:TPU:1, one launch (start us, length us, event | category | flops | bytes accessed | tf_op | source)
XLA Modules:
  0.0 576.0 jit_solution(9939816538325318479)
XLA Ops:
  0.7 62.8 %k1.1 = bf16[1024,512]{1,0:T(8,128)(2,1)} custom-call(bf16[8,16384]{1,0:T(8,128)(2,1)} %ll_ref.1, s32[128,512]{1,0:T(8,128)} %bitcast.87), custom_call_target="tpu_custom_call" | custom-call | tf_op jit(solution)/shard_map/k1/pallas_call | solution.py:89
  63.5 11.5 %all-to-all-start = ((bf16[128,8,512]{2,1,0:T(8,128)(2,1)}), bf16[128,8,512]{2,1,0:T(8,128)(2,1)S(1)}, u32[]{:S(2)}, u32[]{:S(2)}) async-start(bf16[128,8,512]{2,1,0:T(8,128)(2,1)} %bitcast.67), calls=%async_computation | async-start | bytes 2097152 | tf_op jit(solution)/shard_map/all_to_all | solution.py:253
  75.0 1.6 copy.70
  77.3 16.9 %all-to-all-done = bf16[128,8,512]{2,1,0:T(8,128)(2,1)S(1)} async-done(((bf16[128,8,512]{2,1,0:T(8,128)(2,1)}), bf16[128,8,512]{2,1,0:T(8,128)(2,1)S(1)}, u32[]{:S(2)}, u32[]{:S(2)}) %all-to-all-start) | async-done | bytes 1048608 | tf_op jit(solution)/shard_map/all_to_all | solution.py:253
  94.2 1.0 copy-done.3
  95.2 41.9 %k2.1 = bf16[8,4096]{1,0:T(8,128)(2,1)} custom-call(bf16[1024,512]{1,0:T(8,128)(2,1)} %bitcast.66, s32[4,4096]{1,0:T(4,128)} %slot_ref.2, f32[4,4096]{1,0:T(4,128)} %w_ref.2), custom_call_target="tpu_custom_call" | custom-call | tf_op jit(solution)/shard_map/k2/pallas_call | solution.py:109
  137.0 0.9 fusion.19
  138.1 1.0 collective-permute-start.1
  142.1 1.0 collective-permute-start.3
  143.2 2.0 collective-permute-start.2
  145.1 1.0 pad_maximum_fusion.3
  146.4 2.8 collective-permute-done.2
  149.3 0.9 pad_maximum_fusion.1
  150.2 1.1 pad_maximum_fusion.2
  151.7 0.8 bitcast_dynamic-update-slice_fusion
  153.9 7.6 %copy.73 = bf16[8,9,4096]{1,0,2:T(8,128)(2,1)} copy(bf16[8,9,4096]{2,0,1:T(8,128)(2,1)S(1)} %constant_dynamic-update-slice_fusion) | data formatting | bytes 1179648 | tf_op jit(solution)/shard_map/stack | solution.py:196
  161.5 1.8 scatter_fusion
  163.4 9.3 %reshape.110 = bf16[72,4096]{0,1:T(8,128)(2,1)S(1)} reshape(bf16[8,9,4096]{1,0,2:T(8,128)(2,1)} %scatter_fusion) | data formatting | bytes 1179648 | tf_op jit(solution)/shard_map/reshape | solution.py:203
  173.9 1.5 fusion
  176.7 17.5 %k3.1 = bf16[1024,512]{1,0:T(8,128)(2,1)} custom-call(bf16[8,4096]{1,0:T(8,128)(2,1)} %fusion.2.ho_ref, s32[128,512]{1,0:T(8,128)} %bitcast.76), custom_call_target="tpu_custom_call" | custom-call | tf_op jit(solution)/shard_map/k3/pallas_call | solution.py:132
  194.2 31.1 %all_to_all.49 = bf16[128,8,512]{2,1,0:T(8,128)(2,1)} all-to-all(bf16[128,8,512]{2,1,0:T(8,128)(2,1)} %bitcast.68), channel_id=1, replica_groups=mesh['cells'=128] {'cells'}, dimensions={0} | all-to-all | bytes 2097152 | tf_op jit(solution)/shard_map/all_to_all | solution.py:265
  225.3 261.9 %k4.1 = (bf16[8,16384]{1,0:T(8,128)(2,1)}, bf16[1024,512]{1,0:T(8,128)(2,1)}) custom-call(bf16[1024,512]{1,0:T(8,128)(2,1)} %bitcast.65, bf16[8,16384]{1,0:T(8,128)(2,1)} %tgt_ref.1, s32[4,16384]{1,0:T(4,128)} %slot_ref.3, f32[4,16384]{1,0:T(4,128)} %w_ref.3), custom_call_target="tpu_custom_call" | custom-call | tf_op jit(solution)/shard_map/k4/pallas_call | solution.py:57
  487.2 24.7 %all_to_all.50 = bf16[128,8,512]{2,1,0:T(8,128)(2,1)} all-to-all(bf16[128,8,512]{2,1,0:T(8,128)(2,1)} %bitcast.75), channel_id=1, replica_groups=mesh['cells'=128] {'cells'}, dimensions={0} | all-to-all | bytes 2097152 | tf_op jit(solution)/shard_map/all_to_all | solution.py:267
  511.9 14.9 %k5.1 = bf16[8,4096]{1,0:T(8,128)(2,1)} custom-call(bf16[1024,512]{1,0:T(8,128)(2,1)} %bitcast.69, s32[128,512]{1,0:T(8,128)} %bitcast.77), custom_call_target="tpu_custom_call" | custom-call | tf_op jit(solution)/shard_map/k5/pallas_call | solution.py:162
  526.8 1.1 fusion.22
  527.9 1.2 fusion.21
  529.1 3.8 convolution_bitcast_fusion.2
  532.9 4.2 fusion.9
  537.1 2.5 fusion.10
  539.6 2.3 fusion.13
  542.6 14.8 %all_to_all.51 = f32[128,1,296]{2,1,0:T(1,128)S(1)} all-to-all(f32[128,1,296]{2,1,0:T(1,128)S(1)} %all_to_all.43), channel_id=1, replica_groups=mesh['cells'=128] {'cells'}, dimensions={0} | all-to-all | bytes 303104 | tf_op jit(solution)/shard_map/all_to_all | solution.py:271
  557.6 14.6 %all_to_all.52 = f32[128,1,296]{2,1,0:T(1,128)S(1)} all-to-all(f32[128,1,296]{2,1,0:T(1,128)S(1)} %broadcast_in_dim.28), channel_id=1, replica_groups=mesh['cells'=128] {'cells'}, dimensions={0} | all-to-all | bytes 303104 | tf_op jit(solution)/shard_map/all_to_all | solution.py:272
  (66 shorter events, 13.1 us)
Async XLA Ops:
  0.6 173.3 %copy-start = (bf16[64,256]{1,0:T(8,128)(2,1)S(1)}, bf16[64,256]{1,0:T(8,128)(2,1)}, u32[]{:S(2)}) copy-start(bf16[64,256]{1,0:T(8,128)(2,1)} %param.22) | copy-start | bytes 98308
  0.6 75.9 %copy-start.7 = (s32[4]{0:T(128)S(1)}, s32[4]{0:T(128)}, u32[]{:S(2)}) copy-start(s32[4]{0:T(128)} %constant.30) | copy-start | bytes 52
  63.5 30.7 %all-to-all-start = ((bf16[128,8,512]{2,1,0:T(8,128)(2,1)}), bf16[128,8,512]{2,1,0:T(8,128)(2,1)S(1)}, u32[]{:S(2)}, u32[]{:S(2)}) async-start(bf16[128,8,512]{2,1,0:T(8,128)(2,1)} %bitcast.67), calls=%async_computation | async-start | bytes 2097152 | tf_op jit(solution)/shard_map/all_to_all | solution.py:253
  94.2 1.0 copy-start.3
  138.1 3.1 collective-permute-start.1
  139.2 1.5 collective-permute-start
  142.1 4.3 collective-permute-start.3
  143.2 6.1 %collective-permute-start.2 = (bf16[8,258]{1,0:T(8,128)(2,1)S(1)}, bf16[8,258]{1,0:T(8,128)(2,1)S(1)}, u32[]{:S(2)}, u32[]{:S(2)}) collective-permute-start(bf16[8,258]{1,0:T(8,128)(2,1)S(1)} %get-tuple-element.32), channel_id=1, source_target_pairs={{0,16},{1,17},{2,18},{3,19},{4,20},{5,21},{6,22},{7,23},{8,24},{9,... | collective-permute-start | bytes 12392 | tf_op jit(solution)/shard_map/ppermute | solution.py:176
  163.4 9.3 %copy-start.5 = (bf16[64,72]{1,0:T(8,128)(2,1)S(1)}, bf16[64,72]{1,0:T(8,128)(2,1)}, u32[]{:S(2)}) copy-start(bf16[64,72]{1,0:T(8,128)(2,1)} %param.20) | copy-start | bytes 27652
  163.4 9.8 %copy-start.4 = (bf16[256,64]{0,1:T(8,128)(2,1)S(1)}, bf16[256,64]{0,1:T(8,128)(2,1)}, u32[]{:S(2)}) copy-start(bf16[256,64]{0,1:T(8,128)(2,1)} %param.21) | copy-start | bytes 98308
  173.9 2.0 copy-start.1
  173.9 1.9 copy-start.6
  529.1 3.8 copy-start.2

commit v2 on v0

v2 whole, which is shorter than its diff:
```python
import functools
import math

import jax
import jax.numpy as jnp
from jax import lax
from jax.experimental import pallas as pl
from jax.experimental.pallas import tpu as pltpu
from jax.sharding import PartitionSpec as P

BF = jnp.bfloat16
F32 = jnp.float32
I16 = jnp.int16
I32 = jnp.int32
VARS = 8
GRID_ROWS = 8
TILE_ROWS = 16
TILE_WIDTH = 256

def onehot(h, n):
    it = lax.broadcasted_iota(I16, (n, h.shape[1]), 0)
    hh = jnp.broadcast_to(h.astype(I16), (n, h.shape[1]))
    return jnp.where(it == hh, jnp.ones((), BF), jnp.zeros((), BF))

def picktree(mm, lo, count):
    l8 = jnp.broadcast_to(lo, (8, lo.shape[1]))
    masks = {}
    c = count // 2
    while c:
        masks[c] = (l8 & c) != 0
        c //= 2
    def tree(base, n):
        if n == 1: return mm[8*base:8*base+8]
        h = n // 2
        a = tree(base, h); b = tree(base+h, h)
        return jnp.where(masks[h], b, a)
    return tree(0, count)

def k4d_body(BP, tab_ref, tgt_ref, slot_ref, w_ref, pred_ref, send_ref, oh_ref, acc_ref):
    i = pl.program_id(0)
    scale = 1.0 / math.sqrt(2097152)
    @pl.when(i == 0)
    def _(): acc_ref[...] = jnp.zeros_like(acc_ref)
    p = jnp.zeros((8, BP), F32)
    for t in range(4):
        idx = slot_ref[t:t+1, :]
        oh = onehot(idx & 511, 512)
        oh_ref[:, t*BP:(t+1)*BP] = oh
        mm = jnp.dot(tab_ref[...], oh, preferred_element_type=F32)
        p = p + w_ref[t:t+1, :] * picktree(mm, idx >> 9, 128)
    pb = p.astype(BF)
    pred_ref[...] = pb
    g = (pb.astype(F32) - tgt_ref[...].astype(F32)) * scale
    half = lax.broadcasted_iota(I16, (16, 4*BP), 0) >> 3
    z = jnp.zeros((), BF)
    val = jnp.concatenate([(w_ref[t:t+1, :] * g).astype(BF) for t in range(4)], axis=1)
    d = jnp.concatenate([slot_ref[t:t+1, :] >> 9 for t in range(4)], axis=1)
    val2 = jnp.concatenate([val, val], axis=0)
    q = jnp.broadcast_to(d.astype(I16), (16, 4*BP)) - half
    e = jnp.concatenate([jnp.where(q == jnp.int16(2*k), val2, z) for k in range(64)], axis=0)
    acc_ref[...] += lax.dot_general(e, oh_ref[...], (((1,), (1,)), ((), ())), preferred_element_type=F32)
    @pl.when(i == pl.num_programs(0)-1)
    def _(): send_ref[...] = acc_ref[...].astype(BF)

def k2c_body(BC, tab_ref, slot_ref, w_ref, out_ref):
    p = jnp.zeros((8, BC), F32)
    for t in range(4):
        idx = slot_ref[t:t+1, :]
        mm = jnp.dot(tab_ref[...], onehot(idx & 511, 512), preferred_element_type=F32)
        p = p + w_ref[t:t+1, :] * picktree(mm, idx >> 9, 128)
    out_ref[...] = p.astype(BF)

def k2c(tab, slot, w, BC=512):
    return pl.pallas_call(functools.partial(k2c_body, BC), grid=(4096//BC,),
        in_specs=[pl.BlockSpec((1024,512), lambda i:(0,0)), pl.BlockSpec((4,BC), lambda i:(0,i)), pl.BlockSpec((4,BC), lambda i:(0,i))],
        out_specs=pl.BlockSpec((8,BC), lambda i:(0,i)),
        out_shape=jax.ShapeDtypeStruct((8,4096), BF), name="k2")(tab, slot, w)

def k1c_body(ll_ref, rows_ref, out_ref, tab_ref):
    @pl.when(pl.program_id(0) == 0)
    def _():
        for k in range(16):
            a = ll_ref[:, 1024*k:1024*k+512]; b = ll_ref[:, 1024*k+512:1024*k+1024]
            tab_ref[16*k:16*k+16, :] = jnp.concatenate([a, b], axis=0)
    for j in range(4):
        outs = []
        for u in range(2):
            idx = rows_ref[2*j+u:2*j+u+1, :]
            mm = jnp.dot(tab_ref[...], onehot(idx & 511, 512), preferred_element_type=F32)
            outs.append(picktree(mm, idx >> 9, 32))
        out_ref[16*j:16*j+16, :] = jnp.concatenate(outs, 0).astype(BF)

def k1c(ll, rows):
    return pl.pallas_call(k1c_body, grid=(16,),
        in_specs=[pl.BlockSpec((8,16384), lambda i:(0,0)), pl.BlockSpec((8,512), lambda i:(i,0))],
        out_specs=pl.BlockSpec((64,512), lambda i:(i,0)),
        out_shape=jax.ShapeDtypeStruct((1024,512), BF),
        scratch_shapes=[pltpu.VMEM((256,512), BF)], name="k1")(ll, rows)

def mk4(body, ohs, BP):
    def k4(tab, target, slot, w):
        points = target.shape[1]
        return pl.pallas_call(
            functools.partial(body, BP),
            grid=(points//BP,),
            in_specs=[pl.BlockSpec((1024,512), lambda i:(0,0)), pl.BlockSpec((8,BP), lambda i:(0,i)),
                      pl.BlockSpec((4,BP), lambda i:(0,i)), pl.BlockSpec((4,BP), lambda i:(0,i))],
            out_specs=[pl.BlockSpec((8,BP), lambda i:(0,i)), pl.BlockSpec((1024,512), lambda i:(0,0))],
            out_shape=[jax.ShapeDtypeStruct((8,points), BF), jax.ShapeDtypeStruct((1024,512), BF)],
            scratch_shapes=[pltpu.VMEM(ohs, BF), pltpu.VMEM((1024,512), F32)],
            name="k4",
        )(tab, target, slot, w)
    return k4

def kf_body(reg_ref, lc_ref, rc_ref, up_ref, lw_ref, n0_ref, n1_ref, n2_ref, n3_ref, cw_ref, uw_ref, dw_ref, hw_ref, rows_ref,
            out_ref, st_ref, tab_ref):
    @pl.when(pl.program_id(0) == 0)
    def _():
        w = 256
        reg = reg_ref[...].astype(F32)
        pick_col = (lax.broadcasted_iota(I32, (16, 4096), 1) == 256 * lax.broadcasted_iota(I32, (16, 4096), 0))
        spread = jnp.where(pick_col, 1.0, 0.0).astype(BF)
        lcol = jnp.dot(lc_ref[...], spread, preferred_element_type=F32)
        rcol = pltpu.roll(jnp.dot(rc_ref[...], spread, preferred_element_type=F32), 255, 1)
        col = lax.broadcasted_iota(I32, (8, 4096), 1) & 255
        left = jnp.where(col == 0, lcol, pltpu.roll(reg, 1, 1))
        right = jnp.where(col == 255, rcol, pltpu.roll(reg, 4095, 1))
        def line(ref, swap_l, swap_r):
            x = ref[...].astype(F32)
            a, b, c = x[:, 0:w], x[:, 1:w+1], x[:, 2:w+2]
            lane = lax.broadcasted_iota(I32, (8, w), 1)
            a = jnp.where((lane == 0) & swap_l, b, a)
            c = jnp.where((lane == w-1) & swap_r, b, c)
            return a, b, c
        ups = line(up_ref, n0_ref[0:1, 0:1] != 0, n1_ref[2:3, 127:128] != 257)
        lows = line(lw_ref, n2_ref[6:7, 0:1] != 17*258, n3_ref[8:9, 127:128] != 17*258+257)
        for dc, mid in enumerate((left, reg, right)):
            full = jnp.concatenate([ups[dc], mid, lows[dc]], axis=1).astype(BF)
            for dr in range(3):
                st_ref[(dr*3+dc)*8:(dr*3+dc)*8+8, :] = full[:, dr*w:dr*w+4096]
        def chunk(j, c):
            s = st_ref[:, pl.ds(pl.multiple_of(j*512, 512), 512)]
            conv = jnp.dot(cw_ref[...], s, preferred_element_type=F32)
            pre = jnp.dot(uw_ref[...], conv.astype(BF), preferred_element_type=F32)
            act = jax.nn.gelu(pre).astype(BF)
            mixed = (conv + jnp.dot(dw_ref[...], act, preferred_element_type=F32)).astype(BF)
            head = jnp.dot(hw_ref[...], mixed, preferred_element_type=F32).astype(BF)
            tab_ref[pl.ds(pl.multiple_of(16*j,16),16), :] = jnp.concatenate([head[:, :256], head[:, 256:]], axis=0)
            return c
        lax.fori_loop(0, 8, chunk, 0)
    for j in range(8):
        outs = []
        for u in range(2):
            idx = rows_ref[2*j+u:2*j+u+1, :]
            mm = jnp.dot(tab_ref[...], onehot(idx & 255, 256), preferred_element_type=F32)
            outs.append(picktree(mm, idx >> 8, 16))
        out_ref[16*j:16*j+16, :] = jnp.concatenate(outs, 0).astype(BF)

def kf(reg, lc, rc, up, lw, neigh, cw, uw, dw, hw, rows):
    fix = lambda s: pl.BlockSpec(s, lambda i: (0, 0))
    nb = lambda b: pl.BlockSpec((9, 128), lambda i: (0, b))
    return pl.pallas_call(kf_body, grid=(8,),
        in_specs=[fix((8,4096)), fix((8,16)), fix((8,16)), fix((8,258)), fix((8,258)), nb(0), nb(1), nb(30), nb(31),
                  fix((64,72)), fix((256,64)), fix((64,256)), fix((8,64)), pl.BlockSpec((16,512), lambda i:(i,0))],
        out_specs=[pl.BlockSpec((128,512), lambda i:(i,0)), fix((72,4096))],
        out_shape=[jax.ShapeDtypeStruct((1024,512), BF), jax.ShapeDtypeStruct((72,4096), BF)],
        scratch_shapes=[pltpu.VMEM((128,256), BF)], name="kf",
    )(reg, lc, rc, up, lw, neigh, neigh, neigh, neigh, cw, uw, dw, hw, rows)

def gelu_both(x):
    c = math.sqrt(2 / math.pi)
    x2 = x * x
    th = jnp.tanh(c * (x + 0.044715 * x2 * x))
    act = x * (0.5 * (1.0 + th))
    der = 0.5 * (1.0 + th) + 0.5 * x * (1.0 - th * th) * (c * (1.0 + 3 * 0.044715 * x2))
    return act, der

def nt(a, b):
    return lax.dot_general(a, b, (((1,), (1,)), ((), ())), preferred_element_type=F32)

def kb_body(sg_ref, rows_ref, st_ref, cw_ref, uw_ref, dw_ref, hw_ref, ut_ref, dt_ref, ht_ref,
            gc_ref, gu_ref, gd_ref, gh_ref, acc_ref):
    i = pl.program_id(0)
    @pl.when(i == 0)
    def _(): acc_ref[...] = jnp.zeros_like(acc_ref)
    half = lax.broadcasted_iota(I16, (16, 4096), 0) >> 3
    z = jnp.zeros((), BF)
    val = jnp.concatenate([sg_ref[8*j:8*j+8, :] for j in range(8)], axis=1)
    idx = jnp.concatenate([rows_ref[j:j+1, :] for j in range(8)], axis=1)
    val2 = jnp.concatenate([val, val], axis=0)
    q = jnp.broadcast_to((idx >> 8).astype(I16), (16, 4096)) - half
    e = jnp.concatenate([jnp.where(q == jnp.int16(2*k), val2, z) for k in range(8)], axis=0)
    acc_ref[...] += nt(e, onehot(idx & 255, 256))
    @pl.when(i == pl.num_programs(0)-1)
    def _():
        gc_ref[...] = jnp.zeros_like(gc_ref); gu_ref[...] = jnp.zeros_like(gu_ref)
        gd_ref[...] = jnp.zeros_like(gd_ref); gh_ref[...] = jnp.zeros_like(gh_ref)
        def chunk(j, c):
            s = st_ref[:, pl.ds(pl.multiple_of(j*512, 512), 512)]
            a2 = acc_ref[pl.ds(pl.multiple_of(16*j,16),16), :]
            go = jnp.concatenate([a2[:8], a2[8:]], axis=1).astype(BF)
            conv = jnp.dot(cw_ref[...], s, preferred_element_type=F32)
            cb = conv.astype(BF)
            pre = jnp.dot(uw_ref[...], cb, preferred_element_type=F32)
            act, der = gelu_both(pre)
            act = act.astype(BF)
            mixed = (conv + jnp.dot(dw_ref[...], act, preferred_element_type=F32)).astype(BF)
            gm = jnp.dot(ht_ref[...], go, preferred_element_type=F32)
            gmb = gm.astype(BF)
            gh_ref[...] += nt(go, mixed)
            gp = (jnp.dot(dt_ref[...], gmb, preferred_element_type=F32) * der).astype(BF)
            gd_ref[...] += nt(gmb, act)
            gu_ref[...] += nt(gp, cb)
            gco = (gm + jnp.dot(ut_ref[...], gp, preferred_element_type=F32)).astype(BF)
            gc_ref[...] += nt(gco, s)
            return c
        lax.fori_loop(0, 8, chunk, 0)

def kb(sg, rows, st, cw, uw, dw, hw):
    fix = lambda s: pl.BlockSpec(s, lambda i: (0, 0))
    return pl.pallas_call(kb_body, grid=(16,),
        in_specs=[pl.BlockSpec((64,512), lambda i:(i,0)), pl.BlockSpec((8,512), lambda i:(i,0)), fix((72,4096)),
                  fix((64,72)), fix((256,64)), fix((64,256)), fix((8,64)), fix((64,256)), fix((256,64)), fix((64,8))],
        out_specs=[fix((64,72)), fix((256,64)), fix((64,256)), fix((8,64))],
        out_shape=[jax.ShapeDtypeStruct(s, F32) for s in ((64,72), (256,64), (64,256), (8,64))],
        scratch_shapes=[pltpu.VMEM((128,256), F32)], name="kb",
    )(sg, rows, st, cw, uw, dw, hw, uw.T, dw.T, hw.T)

k4d = mk4(k4d_body, (512, 2048), 512)


def from_behind(value, by):
    devices = lax.axis_size("cells")
    return lax.ppermute(value, "cells", [(i, (i + by) % devices) for i in range(devices)])


def body(
    ll_fields, target, in_rows, in_slot, in_weight, neighbours, conv_weight, up_weight, down_weight,
    head_weight, out_rows, out_slot, out_weight,
):
    devices = lax.axis_size("cells")
    tile_cols = devices // GRID_ROWS
    exchange = functools.partial(
        lax.all_to_all, axis_name="cells", split_axis=0, concat_axis=0, tiled=True
    )
    received = exchange(k1c(ll_fields, in_rows[0]))
    flat_reg = k2c(received, in_slot, in_weight)
    regridded = flat_reg.reshape(VARS, TILE_ROWS, TILE_WIDTH)
    left_col = from_behind(regridded[:, :, TILE_WIDTH - 1], 1)
    right_col = from_behind(regridded[:, :, 0], -1)
    last, first = TILE_ROWS - 1, 0
    line = lambda r: jnp.concatenate(
        [left_col[:, r : r + 1], regridded[:, r, :], right_col[:, r : r + 1]], axis=1
    )
    upper_line = from_behind(line(last), tile_cols)
    lower_line = from_behind(line(first), -tile_cols)
    conv_w = conv_weight.reshape(64, VARS, 9).transpose(0, 2, 1).reshape(64, 72)
    sending, stacked = kf(
        flat_reg, left_col, right_col, upper_line, lower_line, neighbours, conv_w, up_weight,
        down_weight, head_weight, out_rows[0],
    )
    arrived = exchange(sending)
    predicted, slot_grad = k4d(arrived, target, out_slot, out_weight)
    returned = exchange(slot_grad)
    terms = kb(returned, out_rows[0], stacked, conv_w, up_weight, down_weight, head_weight)
    flat = jnp.concatenate([term.reshape(-1) for term in terms]).reshape(devices, -1)
    part = jnp.sum(exchange(flat), axis=0, keepdims=True)
    whole = exchange(jnp.broadcast_to(part, flat.shape)).reshape(-1)
    totals, at = [], 0
    for term in terms:
        totals.append(whole[at : at + term.size].reshape(term.shape))
        at += term.size
    totals[0] = totals[0].reshape(64, 9, VARS).transpose(0, 2, 1).reshape(64, 72)
    return (predicted, *totals)


def solution(mesh):
    placed = (
        P(None, "cells"),
        P(None, "cells"),
        P("cells", None, None),
        P(None, "cells"),
        P(None, "cells"),
        P(None, "cells"),
        P(),
        P(),
        P(),
        P(),
        P("cells", None, None),
        P(None, "cells"),
        P(None, "cells"),
    )
    return jax.shard_map(
        body,
        mesh=mesh,
        in_specs=placed,
        out_specs=(P(None, "cells"), P(), P(), P(), P()),
        check_vma=False,
    )
```

time: 1990 us -> 376 us (0.19)
  local copies, waits for them, and re-layouts: 951 us -> 14.9 us
  other arithmetic: 793 us -> 0.8 us
  Pallas kernels: 0 us -> 234 us
  waiting for transfers between devices: 111 us -> 18.3 us
  blocking collectives: 63.3 us -> 93.9 us
  starting transfers between devices: 37.7 us -> 11.2 us
    gather x20 -> x0, local copies, waits for them, and re-layouts: 834 us -> none  [the longest x12 356 us: spread_taps(): flattened[:, slot_table[tap_index]].astype(jnp.float32)]
    scatter-add x5 -> x0, other arithmetic: 750 us -> none  [the longest x4 402 us: body(): slot_grad.at[:, out_slot[tap_index]].add(out_weight[tap_index] * grad_pred)]
    pallas_call x0 -> x5, Pallas kernels: none -> 234 us  [the longest x1 153 us: k4(): pl.pallas_call(functools.partial(body, BP), grid=(points // BP,), in_spec...]
    all_to_all x0 -> x4, blocking collectives: none -> 93.9 us  [the longest x1 33.7 us: body(): arrived = exchange(sending)]
    psum x1 -> x0, waiting for transfers between devices: 74.9 us -> none  [body(): totals = lax.psum((terms[0], terms[1], terms[2], terms[3]), 'cells')]
    psum x1 -> x0, blocking collectives: 63.3 us -> none  [body(): totals = lax.psum((terms[0], terms[1], terms[2], terms[3]), 'cells')]
    all_to_all x3 -> x1, starting transfers between devices: 30.2 us -> 4.28 us  [body(): returned = exchange(slot_grad)]
    mul x8 -> x0, local copies, waits for them, and re-layouts: 24.1 us -> none  [the longest x4 20.8 us: body(): out_weight[tap_index] * grad_pred]
  transfers between devices with their start and end apart: 8 -> 5, of which waited for: 4 -> 2; matrix products, arithmetic and copies ran while one was open for 1% -> 1% of each run, Pallas kernels for 0% -> 0%
where the time goes in v2:
time: 376 us; the launch traced here: 374 us
  Pallas kernels  234 us (62%)
  blocking collectives  93.9 us (25%)
  waiting for transfers between devices  18.3 us (5%)
  local copies, waits for them, and re-layouts  14.9 us (4%)
  starting transfers between devices  11.2 us (3%)
    pallas_call x1, Pallas kernels, k4(): pl.pallas_call(functools.partial(body, BP), grid=(points // BP,), in_spec...  153 us
    all_to_all x1, blocking collectives, body(): arrived = exchange(sending)  33.7 us
    all_to_all x1, blocking collectives, body(): received = exchange(k1c(ll_fields, in_rows[0]))  30.8 us
    pallas_call x1, Pallas kernels, kb(): pl.pallas_call(kb_body, grid=(16,), in_specs=[pl.BlockSpec((64, 512), lam...  24.3 us
    pallas_call x1, Pallas kernels, k1c(): pl.pallas_call(k1c_body, grid=(16,), in_specs=[pl.BlockSpec((8, 16384), l...  22.2 us
    pallas_call x1, Pallas kernels, k2c(): pl.pallas_call(functools.partial(k2c_body, BC), grid=(4096 // BC,), in_sp...  20.9 us
    all_to_all x1, waiting for transfers between devices, body(): returned = exchange(slot_grad)  17.9 us
    all_to_all x1, blocking collectives, body(): part = jnp.sum(exchange(flat), axis=0, keepdims=True)  14.8 us
  transfers between devices with their start and end apart: 5, of which 2 were waited for; matrix products, arithmetic and copies ran while one was open for 1% of the time, Pallas kernels for 0%

profile of v2, /device:TPU:1, one launch (start us, length us, event | category | flops | bytes accessed | tf_op | source)
XLA Modules:
  0.0 373.9 jit_solution(6932091259856657096)
XLA Ops:
  0.6 22.2 %k1.1 = bf16[1024,512]{1,0:T(8,128)(2,1)} custom-call(bf16[8,16384]{1,0:T(8,128)(2,1)} %ll_ref.1, s32[128,512]{1,0:T(8,128)} %bitcast.42), custom_call_target="tpu_custom_call" | custom-call | tf_op jit(solution)/shard_map/k1/pallas_call | solution.py:94
  22.9 30.8 %all_to_all.49 = bf16[128,8,512]{2,1,0:T(8,128)(2,1)} all-to-all(bf16[128,8,512]{2,1,0:T(8,128)(2,1)} %bitcast.32), channel_id=1, replica_groups=mesh['cells'=128] {'cells'}, dimensions={0} | all-to-all | bytes 2097152 | tf_op jit(solution)/shard_map/all_to_all | solution.py:246
  53.7 20.9 %k2.1.reg_ref = bf16[8,4096]{1,0:T(8,128)(2,1)} custom-call(bf16[1024,512]{1,0:T(8,128)(2,1)} %bitcast.31, s32[4,4096]{1,0:T(4,128)} %slot_ref.2, f32[4,4096]{1,0:T(4,128)} %w_ref.2), custom_call_target="tpu_custom_call" | custom-call | tf_op jit(solution)/shard_map/k2/pallas_call | solution.py:74
  74.5 0.9 fusion
  75.5 1.0 collective-permute-start.1
  76.5 0.7 slice_bitcast_fusion
  77.4 0.8 collective-permute-start
  78.7 0.5 copy-done.7
  79.3 0.5 copy-done.8
  79.8 0.7 collective-permute-start.2
  80.6 4.4 %collective-permute-start.3 = (bf16[8,258]{1,0:T(8,128)(2,1)S(1)}, bf16[8,258]{1,0:T(8,128)(2,1)S(1)}, u32[]{:S(2)}, u32[]{:S(2)}) collective-permute-start(bf16[8,258]{1,0:T(8,128)(2,1)S(1)} %pad_maximum_fusion.2), channel_id=1, source_target_pairs={{0,112},{1,113},{2,114},{3,115},{4,116},{5,117},{6,118},{7,119},{8... | collective-permute-start | bytes 12392 | tf_op jit(solution)/shard_map/ppermute | solution.py:234
  85.2 0.7 copy.43.cw_ref
  85.9 0.7 copy.44.uw_ref
  86.7 0.6 copy-done.10
  87.2 13.9 %kf.1 = (bf16[1024,512]{1,0:T(8,128)(2,1)}, bf16[72,4096]{1,0:T(8,128)(2,1)}) custom-call(bf16[8,4096]{1,0:T(8,128)(2,1)} %k2.1.reg_ref, bf16[8,16]{1,0:T(8,128)(2,1)} %copy-done.8, bf16[8,16]{1,0:T(8,128)(2,1)} %copy-done.7, bf16[8,258]{1,0:T(8,128)(2,1)} %copy-done.10, bf16[8,258]{1,0:T(8,128)(2,1)} %copy-done.11, s32[9,4096]{1,0:T(8,128)} %n3_ref.1, ...), custom_call_target="tpu_custom_call" | custom-call | tf_op jit(solution)/shard_map/kf/pallas_call | solution.py:162
  101.2 33.7 %all_to_all.50 = bf16[128,8,512]{2,1,0:T(8,128)(2,1)} all-to-all(bf16[128,8,512]{2,1,0:T(8,128)(2,1)} %bitcast.35), channel_id=1, replica_groups=mesh['cells'=128] {'cells'}, dimensions={0} | all-to-all | bytes 2097152 | tf_op jit(solution)/shard_map/all_to_all | solution.py:262
  134.9 152.6 %k4.1 = (bf16[8,16384]{1,0:T(8,128)(2,1)}, bf16[1024,512]{1,0:T(8,128)(2,1)}) custom-call(bf16[1024,512]{1,0:T(8,128)(2,1)} %bitcast.30, bf16[8,16384]{1,0:T(8,128)(2,1)} %tgt_ref.1, s32[4,16384]{1,0:T(4,128)} %slot_ref.3, f32[4,16384]{1,0:T(4,128)} %w_ref.3), custom_call_target="tpu_custom_call" | custom-call | tf_op jit(solution)/shard_map/k4/pallas_call | solution.py:103
  287.4 4.3 %all-to-all-start.2 = ((bf16[128,8,512]{2,1,0:T(8,128)(2,1)}), bf16[128,8,512]{2,1,0:T(8,128)(2,1)S(1)}, u32[]{:S(2)}, u32[]{:S(2)}) async-start(bf16[128,8,512]{2,1,0:T(8,128)(2,1)} %bitcast.34), calls=%async_computation.2 | async-start | bytes 2097152 | tf_op jit(solution)/shard_map/all_to_all | solution.py:264
  291.7 0.7 copy.45
  292.5 0.7 copy.46
  293.2 17.9 %all-to-all-done.2 = bf16[128,8,512]{2,1,0:T(8,128)(2,1)S(1)} async-done(((bf16[128,8,512]{2,1,0:T(8,128)(2,1)}), bf16[128,8,512]{2,1,0:T(8,128)(2,1)S(1)}, u32[]{:S(2)}, u32[]{:S(2)}) %all-to-all-start.2) | async-done | bytes 1048608 | tf_op jit(solution)/shard_map/all_to_all | solution.py:264
  311.1 1.0 copy-done
  312.1 24.3 %kb.1 = (f32[64,72]{1,0:T(8,128)}, f32[256,64]{1,0:T(8,128)}, f32[64,256]{1,0:T(8,128)}, f32[8,64]{1,0:T(8,128)}) custom-call(bf16[1024,512]{1,0:T(8,128)(2,1)} %bitcast.29, s32[128,512]{1,0:T(8,128)} %bitcast.37, bf16[72,4096]{1,0:T(8,128)(2,1)} %get-tuple-element.16.st_ref, bf16[64,72]{1,0:T(8,128)(2,1)} %copy.43.cw_ref, bf16[256,64]{1,0:T(8,128)(2,1)} %copy.44.uw_ref, ...), custom_call_target="tpu_custom_call" | custom-call | tf_op jit(solution)/shard_map/kb/pallas_call | solution.py:221
  336.4 0.8 reshape.69
  337.2 0.9 copy.53
  338.2 0.7 copy-done.5
  339.3 14.8 %all_to_all.51 = f32[128,1,296]{2,1,0:T(1,128)S(1)} all-to-all(f32[128,1,296]{2,1,0:T(1,128)S(1)} %all_to_all.43), channel_id=1, replica_groups=mesh['cells'=128] {'cells'}, dimensions={0} | all-to-all | bytes 303104 | tf_op jit(solution)/shard_map/all_to_all | solution.py:267
  354.3 14.6 %all_to_all.52 = f32[128,1,296]{2,1,0:T(1,128)S(1)} all-to-all(f32[128,1,296]{2,1,0:T(1,128)S(1)} %broadcast_in_dim.2), channel_id=1, replica_groups=mesh['cells'=128] {'cells'}, dimensions={0} | all-to-all | bytes 303104 | tf_op jit(solution)/shard_map/all_to_all | solution.py:268
  370.6 0.6 slice.64
  371.6 0.7 copy.51
  372.5 0.7 copy.52
  373.2 0.6 slice.63
  (48 shorter events, 4.1 us)
Async XLA Ops:
  75.5 3.1 collective-permute-start.1
  77.4 1.8 collective-permute-start
  78.6 0.6 copy-start.7
  79.2 0.6 copy-start.8
  79.8 5.2 %copy-start.9 = (bf16[64,72]{1,0:T(8,128)(2,1)S(1)}, bf16[64,72]{1,0:T(8,128)(2,1)}, u32[]{:S(2)}) copy-start(bf16[64,72]{1,0:T(8,128)(2,1)} %param.19) | copy-start | bytes 27652
  79.8 6.8 %collective-permute-start.2 = (bf16[8,258]{1,0:T(8,128)(2,1)S(1)}, bf16[8,258]{1,0:T(8,128)(2,1)S(1)}, u32[]{:S(2)}, u32[]{:S(2)}) collective-permute-start(bf16[8,258]{1,0:T(8,128)(2,1)S(1)} %pad_maximum_fusion.1), channel_id=1, source_target_pairs={{0,16},{1,17},{2,18},{3,19},{4,20},{5,21},{6,22},{7,23},{8,24},{9,... | collective-permute-start | bytes 12392 | tf_op jit(solution)/shard_map/ppermute | solution.py:234
  80.6 6.0 %collective-permute-start.3 = (bf16[8,258]{1,0:T(8,128)(2,1)S(1)}, bf16[8,258]{1,0:T(8,128)(2,1)S(1)}, u32[]{:S(2)}, u32[]{:S(2)}) collective-permute-start(bf16[8,258]{1,0:T(8,128)(2,1)S(1)} %pad_maximum_fusion.2), channel_id=1, source_target_pairs={{0,112},{1,113},{2,114},{3,115},{4,116},{5,117},{6,118},{7,119},{8... | collective-permute-start | bytes 12392 | tf_op jit(solution)/shard_map/ppermute | solution.py:234
  85.1 0.8 copy-start.3
  86.6 0.6 copy-start.10
  86.6 0.6 copy-start.11
  287.4 4.3 %copy-start.2 = (bf16[64,256]{1,0:T(8,128)(2,1)S(1)}, bf16[64,256]{1,0:T(8,128)(2,1)}, u32[]{:S(2)}) copy-start(bf16[64,256]{1,0:T(8,128)(2,1)} %dw_ref.3) | copy-start | bytes 98308
  287.4 23.6 %all-to-all-start.2 = ((bf16[128,8,512]{2,1,0:T(8,128)(2,1)}), bf16[128,8,512]{2,1,0:T(8,128)(2,1)S(1)}, u32[]{:S(2)}, u32[]{:S(2)}) async-start(bf16[128,8,512]{2,1,0:T(8,128)(2,1)} %bitcast.34), calls=%async_computation.2 | async-start | bytes 2097152 | tf_op jit(solution)/shard_map/all_to_all | solution.py:264
  291.7 0.7 copy-start.6
  311.1 1.0 copy-start
  336.4 1.7 copy-start.4
  338.1 0.8 copy-start.5
  369.9 0.7 copy-start.1
  371.6 0.9 slice-start

commit v3 on v2

--- a/solution.py
+++ b/solution.py
@@ -36,46 +36,6 @@
         return jnp.where(masks[h], b, a)
     return tree(0, count)
 
-def k4d_body(BP, tab_ref, tgt_ref, slot_ref, w_ref, pred_ref, send_ref, oh_ref, acc_ref):
-    i = pl.program_id(0)
-    scale = 1.0 / math.sqrt(2097152)
-    @pl.when(i == 0)
-    def _(): acc_ref[...] = jnp.zeros_like(acc_ref)
-    p = jnp.zeros((8, BP), F32)
-    for t in range(4):
-        idx = slot_ref[t:t+1, :]
-        oh = onehot(idx & 511, 512)
-        oh_ref[:, t*BP:(t+1)*BP] = oh
-        mm = jnp.dot(tab_ref[...], oh, preferred_element_type=F32)
-        p = p + w_ref[t:t+1, :] * picktree(mm, idx >> 9, 128)
-    pb = p.astype(BF)
-    pred_ref[...] = pb
-    g = (pb.astype(F32) - tgt_ref[...].astype(F32)) * scale
-    half = lax.broadcasted_iota(I16, (16, 4*BP), 0) >> 3
-    z = jnp.zeros((), BF)
-    val = jnp.concatenate([(w_ref[t:t+1, :] * g).astype(BF) for t in range(4)], axis=1)
-    d = jnp.concatenate([slot_ref[t:t+1, :] >> 9 for t in range(4)], axis=1)
-    val2 = jnp.concatenate([val, val], axis=0)
-    q = jnp.broadcast_to(d.astype(I16), (16, 4*BP)) - half
-    e = jnp.concatenate([jnp.where(q == jnp.int16(2*k), val2, z) for k in range(64)], axis=0)
-    acc_ref[...] += lax.dot_general(e, oh_ref[...], (((1,), (1,)), ((), ())), preferred_element_type=F32)
-    @pl.when(i == pl.num_programs(0)-1)
-    def _(): send_ref[...] = acc_ref[...].astype(BF)
-
-def k2c_body(BC, tab_ref, slot_ref, w_ref, out_ref):
-    p = jnp.zeros((8, BC), F32)
-    for t in range(4):
-        idx = slot_ref[t:t+1, :]
-        mm = jnp.dot(tab_ref[...], onehot(idx & 511, 512), preferred_element_type=F32)
-        p = p + w_ref[t:t+1, :] * picktree(mm, idx >> 9, 128)
-    out_ref[...] = p.astype(BF)
-
-def k2c(tab, slot, w, BC=512):
-    return pl.pallas_call(functools.partial(k2c_body, BC), grid=(4096//BC,),
-        in_specs=[pl.BlockSpec((1024,512), lambda i:(0,0)), pl.BlockSpec((4,BC), lambda i:(0,i)), pl.BlockSpec((4,BC), lambda i:(0,i))],
-        out_specs=pl.BlockSpec((8,BC), lambda i:(0,i)),
-        out_shape=jax.ShapeDtypeStruct((8,4096), BF), name="k2")(tab, slot, w)
-
 def k1c_body(ll_ref, rows_ref, out_ref, tab_ref):
     @pl.when(pl.program_id(0) == 0)
     def _():
@@ -96,21 +56,6 @@
         out_specs=pl.BlockSpec((64,512), lambda i:(i,0)),
         out_shape=jax.ShapeDtypeStruct((1024,512), BF),
         scratch_shapes=[pltpu.VMEM((256,512), BF)], name="k1")(ll, rows)
-
-def mk4(body, ohs, BP):
-    def k4(tab, target, slot, w):
-        points = target.shape[1]
-        return pl.pallas_call(
-            functools.partial(body, BP),
-            grid=(points//BP,),
-            in_specs=[pl.BlockSpec((1024,512), lambda i:(0,0)), pl.BlockSpec((8,BP), lambda i:(0,i)),
-                      pl.BlockSpec((4,BP), lambda i:(0,i)), pl.BlockSpec((4,BP), lambda i:(0,i))],
-            out_specs=[pl.BlockSpec((8,BP), lambda i:(0,i)), pl.BlockSpec((1024,512), lambda i:(0,0))],
-            out_shape=[jax.ShapeDtypeStruct((8,points), BF), jax.ShapeDtypeStruct((1024,512), BF)],
-            scratch_shapes=[pltpu.VMEM(ohs, BF), pltpu.VMEM((1024,512), F32)],
-            name="k4",
-        )(tab, target, slot, w)
-    return k4
 
 def kf_body(reg_ref, lc_ref, rc_ref, up_ref, lw_ref, n0_ref, n1_ref, n2_ref, n3_ref, cw_ref, uw_ref, dw_ref, hw_ref, rows_ref,
             out_ref, st_ref, tab_ref):
@@ -226,7 +171,135 @@
         scratch_shapes=[pltpu.VMEM((128,256), F32)], name="kb",
     )(sg, rows, st, cw, uw, dw, hw, uw.T, dw.T, hw.T)
 
-k4d = mk4(k4d_body, (512, 2048), 512)
+def prep_body(slot_ref, pos_ref, code_ref, gid_ref, ohp_ref):
+    idx = jnp.concatenate([slot_ref[t:t+1, :] for t in range(4)], axis=1)
+    d = idx >> 9
+    g = d >> 4
+    it8 = lax.broadcasted_iota(I32, (8, 256), 0)
+    hot = [jnp.where(it8 == g[:, 256*b:256*b+256], 1.0, 0.0) for b in range(16)]
+    a = jnp.concatenate(hot, axis=0).astype(BF)
+    sq = lambda f, n: jnp.where(f(lax.broadcasted_iota(I32, (n, n), 0), lax.broadcasted_iota(I32, (n, n), 1)), 1.0, 0.0).astype(BF)
+    excl = jnp.dot(a, sq(lambda r, c: r < c, 256), preferred_element_type=F32)
+    tot = jnp.dot(a, jnp.ones((256, 256), BF), preferred_element_type=F32)
+    prefix = jnp.dot(sq(lambda r, c: ((r & 7) == (c & 7)) & (c < (r & ~7)), 128), tot.astype(BF), preferred_element_type=F32)
+    count = prefix[120:128] + tot[120:128]
+    nblk = ((count.astype(I32) + 255) >> 8).astype(F32)
+    both = jnp.concatenate([nblk, jnp.zeros_like(nblk)], axis=0).astype(BF)
+    base = jnp.dot(sq(lambda r, c: c < r, 16), both, preferred_element_type=F32)[:8]
+    lane = lax.broadcasted_iota(I32, (8, 256), 1).astype(F32)
+    gid = jnp.sum(jnp.where(lane >= base + nblk, 1.0, 0.0), axis=0, keepdims=True).astype(I32)
+    gid_ref[0] = jnp.minimum(gid, 7)
+    first = 256.0 * base
+    pos = jnp.concatenate([
+        jnp.sum(hot[b] * (excl[8*b:8*b+8] + prefix[8*b:8*b+8] + first), axis=0, keepdims=True) for b in range(16)
+    ], axis=1).astype(I32)
+    pos_ref[0] = pos
+    ohp_ref[...] = onehot(pos & 255, 256)
+    z = jnp.zeros((), BF)
+    q = jnp.broadcast_to((pos >> 8).astype(I16), (16, 4096)) - lax.broadcasted_iota(I16, (16, 4096), 0)
+    low = jnp.broadcast_to((idx & 255).astype(F32), (16, 4096)).astype(BF)
+    high = jnp.broadcast_to(((idx >> 8) & 31).astype(F32), (16, 4096)).astype(BF)
+    e = jnp.concatenate([jnp.where(q == jnp.int16(16*k), v, z) for v in (low, high) for k in range(2)], axis=0)
+    r = nt(e, ohp_ref[...])
+    code_ref[...] = (r[:32] + 256.0 * r[32:]).astype(I32)
+
+def prep(slot):
+    n = slot.shape[1] // 1024
+    return pl.pallas_call(prep_body, grid=(n,),
+        in_specs=[pl.BlockSpec((4,1024), lambda i:(0,i))],
+        out_specs=[pl.BlockSpec((1,1,4096), lambda i:(i,0,0)), pl.BlockSpec((32,256), lambda i:(i,0)), pl.BlockSpec((1,1,256), lambda i:(i,0,0))],
+        out_shape=[jax.ShapeDtypeStruct((n,1,4096), I32), jax.ShapeDtypeStruct((32*n,256), I32), jax.ShapeDtypeStruct((n,1,256), I32)],
+        scratch_shapes=[pltpu.VMEM((256,4096), BF)], name="prep",
+        cost_estimate=pl.CostEstimate(flops=n*1600000000, bytes_accessed=n*60000, transcendentals=0),
+    )(slot)
+
+def tree24(mm, blk):
+    l8 = jnp.broadcast_to(blk, (8, blk.shape[1]))
+    m = {c: (l8 & c) != 0 for c in (1, 2, 4, 8, 16)}
+    def tree(base, n):
+        if n == 1: return mm[8*base:8*base+8]
+        h = n // 2
+        return jnp.where(m[h], tree(base+h, h), tree(base, h)) if n < 32 else jnp.where(m[16], tree(16, 8), tree(0, 16))
+    return tree(0, 32)
+
+def look_up(i, tab_ref, code_ref, gid_ref, res_ref, oh_ref):
+    for b in range(0, NB, 2):
+        outs = []
+        for u in range(2):
+            code = code_ref[b+u:b+u+1, :]
+            oh = onehot(code & 511, 512)
+            if oh_ref is not None:
+                oh_ref[:, 256*(b+u):256*(b+u+1)] = oh
+            rows = tab_ref[pl.ds(pl.multiple_of(gid_ref[i, b+u] * 128, 128), 128), :]
+            mm = jnp.dot(rows, oh, preferred_element_type=F32)
+            outs.append(picktree(mm, code >> 9, 16))
+        res_ref[8*b:8*b+16, :] = jnp.concatenate(outs, axis=0).astype(BF)
+
+def blend(pos_ref, w_ref, res_ref, ohp_ref, n):
+    p = jnp.zeros((8, n), F32)
+    for t in range(4):
+        pos = pos_ref[0, :, t*n:(t+1)*n]
+        ohp = onehot(pos & 255, 256)
+        if ohp_ref is not None:
+            ohp_ref[:, t*n:(t+1)*n] = ohp
+        mm = jnp.dot(res_ref[...], ohp, preferred_element_type=F32)
+        p = p + w_ref[t:t+1, :] * tree24(mm, pos >> 8)
+    return p
+
+def k4s_body(gid_ref, tab_ref, tgt_ref, w_ref, pos_ref, code_ref, pred_ref, send_ref, res_ref, oh_ref, ohp_ref, acc_ref):
+    i = pl.program_id(0)
+    n = 1024
+    scale = 1.0 / math.sqrt(2097152)
+    @pl.when(i == 0)
+    def _(): acc_ref[...] = jnp.zeros_like(acc_ref)
+    look_up(i, tab_ref, code_ref, gid_ref, res_ref, oh_ref)
+    pb = blend(pos_ref, w_ref, res_ref, ohp_ref, n).astype(BF)
+    pred_ref[...] = pb
+    g = (pb.astype(F32) - tgt_ref[...].astype(F32)) * scale
+    z = jnp.zeros((), BF)
+    val = jnp.concatenate([(w_ref[t:t+1, :] * g).astype(BF) for t in range(4)], axis=1)
+    val2 = jnp.concatenate([val, val], axis=0)
+    half = lax.broadcasted_iota(I16, (16, 4*n), 0) >> 3
+    q = jnp.broadcast_to((pos_ref[0] >> 8).astype(I16), (16, 4*n)) - half
+    e = jnp.concatenate([jnp.where(q == jnp.int16(2*k), val2, z) for k in range(NB//2)], axis=0)
+    sv = nt(e, ohp_ref[...]).astype(BF)
+    half = lax.broadcasted_iota(I16, (16, 256), 0) >> 3
+    for b in range(NB):
+        vb = sv[8*b:8*b+8]
+        v2 = jnp.concatenate([vb, vb], axis=0)
+        q = jnp.broadcast_to((code_ref[b:b+1, :] >> 9).astype(I16), (16, 256)) - half
+        eb = jnp.concatenate([jnp.where(q == jnp.int16(2*k), v2, z) for k in range(8)], axis=0)
+        at = pl.ds(pl.multiple_of(gid_ref[i, b] * 128, 128), 128)
+        acc_ref[at, :] += nt(eb, oh_ref[:, 256*b:256*b+256])
+    @pl.when(i == pl.num_programs(0)-1)
+    def _(): send_ref[...] = acc_ref[...].astype(BF)
+
+def k4s_main(tab, target, w, pos, code, gid):
+    points = target.shape[1]
+    return pl.pallas_call(k4s_body, grid=(points//1024,),
+        in_specs=[pl.BlockSpec(memory_space=pltpu.SMEM), pl.BlockSpec((1024,512), lambda i:(0,0)), pl.BlockSpec((8,1024), lambda i:(0,i)),
+                  pl.BlockSpec((4,1024), lambda i:(0,i)), pl.BlockSpec((1,1,4096), lambda i:(i,0,0)), pl.BlockSpec((32,256), lambda i:(i,0))],
+        out_specs=[pl.BlockSpec((8,1024), lambda i:(0,i)), pl.BlockSpec((1024,512), lambda i:(0,0))],
+        out_shape=[jax.ShapeDtypeStruct((8,points), BF), jax.ShapeDtypeStruct((1024,512), BF)],
+        scratch_shapes=[pltpu.VMEM((8*NB,256), BF), pltpu.VMEM((512,256*NB), BF), pltpu.VMEM((256,4096), BF), pltpu.VMEM((1024,512), F32)],
+        name="k4", compiler_params=pltpu.CompilerParams(vmem_limit_bytes=60*2**20),
+    )(gid.reshape(-1, 256), tab, target, w, pos, code)
+
+def k2s_body(gid_ref, tab_ref, w_ref, pos_ref, code_ref, out_ref, res_ref):
+    look_up(pl.program_id(0), tab_ref, code_ref, gid_ref, res_ref, None)
+    out_ref[...] = blend(pos_ref, w_ref, res_ref, None, 1024).astype(BF)
+
+def k2s_main(tab, w, pos, code, gid):
+    return pl.pallas_call(k2s_body, grid=(4,),
+        in_specs=[pl.BlockSpec(memory_space=pltpu.SMEM), pl.BlockSpec((1024,512), lambda i:(0,0)), pl.BlockSpec((4,1024), lambda i:(0,i)),
+                  pl.BlockSpec((1,1,4096), lambda i:(i,0,0)), pl.BlockSpec((32,256), lambda i:(i,0))],
+        out_specs=pl.BlockSpec((8,1024), lambda i:(0,i)),
+        out_shape=jax.ShapeDtypeStruct((8,4096), BF),
+        scratch_shapes=[pltpu.VMEM((8*NB,256), BF)], name="k2",
+    )(gid.reshape(-1, 256), tab, w, pos, code)
+
+
+NB = 24
 
 
 def from_behind(value, by):
@@ -243,8 +316,10 @@
     exchange = functools.partial(
         lax.all_to_all, axis_name="cells", split_axis=0, concat_axis=0, tiled=True
     )
+    in_plan = prep(in_slot)
+    out_plan = prep(out_slot)
     received = exchange(k1c(ll_fields, in_rows[0]))
-    flat_reg = k2c(received, in_slot, in_weight)
+    flat_reg = k2s_main(received, in_weight, *in_plan)
     regridded = flat_reg.reshape(VARS, TILE_ROWS, TILE_WIDTH)
     left_col = from_behind(regridded[:, :, TILE_WIDTH - 1], 1)
     right_col = from_behind(regridded[:, :, 0], -1)
@@ -260,7 +335,7 @@
         down_weight, head_weight, out_rows[0],
     )
     arrived = exchange(sending)
-    predicted, slot_grad = k4d(arrived, target, out_slot, out_weight)
+    predicted, slot_grad = k4s_main(arrived, target, out_weight, *out_plan)
     returned = exchange(slot_grad)
     terms = kb(returned, out_rows[0], stacked, conv_w, up_weight, down_weight, head_weight)
     flat = jnp.concatenate([term.reshape(-1) for term in terms]).reshape(devices, -1)

time: 376 us -> 306 us (0.81)
  blocking collectives: 93.9 us -> 29.4 us
  Pallas kernels: 234 us -> 182 us
  starting transfers between devices: 11.2 us -> 38.7 us
  waiting for transfers between devices: 18.3 us -> 34 us
  local copies, waits for them, and re-layouts: 14.9 us -> 18.7 us
    all_to_all x2 -> x0, blocking collectives: 64.5 us -> none  [the longest x1 33.7 us: body(): arrived = exchange(sending)]
    pallas_call x2 -> x4, Pallas kernels: 173 us -> 121 us  [the longest x1 85.3 us: k4s_main(): pl.pallas_call(k4s_body, grid=(points // 1024,), in_specs=[pl.BlockSpec(m...]
    all_to_all x0 -> x2, starting transfers between devices: none -> 24.7 us  [the longest x1 13.2 us: body(): arrived = exchange(sending)]
    all_to_all x0 -> x2, waiting for transfers between devices: none -> 11.6 us  [the longest x1 11.6 us: body(): received = exchange(k1c(ll_fields, in_rows[0]))]
    all_to_all x1, starting transfers between devices: 4.28 us -> 9.77 us  [body(): returned = exchange(slot_grad)]
    unnamed x31 -> x37, local copies, waits for them, and re-layouts: 8.35 us -> 13.1 us
    ppermute x4, waiting for transfers between devices: 0.39 us -> 4.64 us  [from_behind(): lax.ppermute(value, 'cells', [(i, (i + by) % devices) for i in range(devi...]
  transfers between devices with their start and end apart: 5 -> 7, of which waited for: 2 -> 4; matrix products, arithmetic and copies ran while one was open for 1% -> 2% of each run, Pallas kernels for 0% -> 9%
where the time goes in v3:
time: 306 us; the launch traced here: 304 us
  Pallas kernels  182 us (59%)
  starting transfers between devices  38.7 us (13%)
  waiting for transfers between devices  34 us (11%)
  blocking collectives  29.4 us (10%)
  local copies, waits for them, and re-layouts  18.7 us (6%)
    pallas_call x1, Pallas kernels, k4s_main(): pl.pallas_call(k4s_body, grid=(points // 1024,), in_specs=[pl.BlockSpec(m...  85.3 us
    pallas_call x2, Pallas kernels, prep(): pl.pallas_call(prep_body, grid=(n,), in_specs=[pl.BlockSpec((4, 1024), la...  27.9 us
    pallas_call x1, Pallas kernels, kb(): pl.pallas_call(kb_body, grid=(16,), in_specs=[pl.BlockSpec((64, 512), lam...  24.3 us
    pallas_call x1, Pallas kernels, k1c(): pl.pallas_call(k1c_body, grid=(16,), in_specs=[pl.BlockSpec((8, 16384), l...  22.2 us
    all_to_all x1, waiting for transfers between devices, body(): returned = exchange(slot_grad)  17.8 us
    all_to_all x1, blocking collectives, body(): part = jnp.sum(exchange(flat), axis=0, keepdims=True)  14.8 us
    all_to_all x1, blocking collectives, body(): whole = exchange(jnp.broadcast_to(part, flat.shape)).reshape(-1)  14.6 us
    pallas_call x1, Pallas kernels, kf(): pl.pallas_call(kf_body, grid=(8,), in_specs=[fix((8, 4096)), fix((8, 16))...  13.9 us
  transfers between devices with their start and end apart: 7, of which 4 were waited for; matrix products, arithmetic and copies ran while one was open for 2% of the time, Pallas kernels for 9%

profile of v3, /device:TPU:1, one launch (start us, length us, event | category | flops | bytes accessed | tf_op | source)
XLA Modules:
  0.0 304.2 jit_solution(6938276230654165050)
XLA Ops:
  0.6 22.2 %k1.1 = bf16[1024,512]{1,0:T(8,128)(2,1)} custom-call(bf16[8,16384]{1,0:T(8,128)(2,1)} %ll_ref.1, s32[128,512]{1,0:T(8,128)} %bitcast.48), custom_call_target="tpu_custom_call" | custom-call | tf_op jit(solution)/shard_map/k1/pallas_call | solution.py:54
  22.9 11.5 %all-to-all-start = ((bf16[128,8,512]{2,1,0:T(8,128)(2,1)}), bf16[128,8,512]{2,1,0:T(8,128)(2,1)S(1)}, u32[]{:S(2)}, u32[]{:S(2)}) async-start(bf16[128,8,512]{2,1,0:T(8,128)(2,1)} %bitcast.38), calls=%async_computation | async-start | bytes 2097152 | tf_op jit(solution)/shard_map/all_to_all | solution.py:321
  34.4 6.4 %prep.3 = (s32[4,1,4096]{2,1,0:T(1,128)}, s32[128,256]{1,0:T(8,128)}, s32[4,1,256]{2,1,0:T(1,128)}) custom-call(s32[4,4096]{1,0:T(4,128)} %slot_ref.3), custom_call_target="tpu_custom_call" | custom-call | flops 6400000000 | bytes 240000 | tf_op jit(solution)/shard_map/prep/pallas_call | solution.py:208
  40.7 1.3 copy.61
  42.0 11.6 %all-to-all-done = bf16[128,8,512]{2,1,0:T(8,128)(2,1)S(1)} async-done(((bf16[128,8,512]{2,1,0:T(8,128)(2,1)}), bf16[128,8,512]{2,1,0:T(8,128)(2,1)S(1)}, u32[]{:S(2)}, u32[]{:S(2)}) %all-to-all-start) | async-done | bytes 1048608 | tf_op jit(solution)/shard_map/all_to_all | solution.py:321
  53.6 1.0 copy-done.2
  54.6 8.1 %k2.1.reg_ref = bf16[8,4096]{1,0:T(8,128)(2,1)} custom-call(s32[4,256]{1,0:T(4,128)} %bitcast.55, bf16[1024,512]{1,0:T(8,128)(2,1)} %bitcast.37, f32[4,4096]{1,0:T(4,128)} %w_ref.2, s32[4,1,4096]{2,1,0:T(1,128)} %get-tuple-element.21.pos_ref, s32[128,256]{1,0:T(8,128)} %get-tuple-element.22.code_ref), custom_call_target="tpu_custom_call" | custom-call | tf_op jit(solution)/shard_map/k2/pallas_call | solution.py:293
  62.7 0.9 fusion
  63.7 1.2 collective-permute-start
  64.8 0.7 slice_bitcast_fusion
  66.3 2.4 collective-permute-done.1.rc_ref
  69.4 0.7 collective-permute-start.3
  70.2 2.2 collective-permute-start.2
  72.6 0.7 copy.43.cw_ref
  73.3 0.7 copy.44.uw_ref
  74.1 2.2 collective-permute-done.2.up_ref
  76.9 13.9 %kf.1 = (bf16[1024,512]{1,0:T(8,128)(2,1)}, bf16[72,4096]{1,0:T(8,128)(2,1)}) custom-call(bf16[8,4096]{1,0:T(8,128)(2,1)} %k2.1.reg_ref, bf16[8,16]{1,0:T(8,128)(2,1)} %copy-done.8, bf16[8,16]{1,0:T(8,128)(2,1)} %copy-done.9, bf16[8,258]{1,0:T(8,128)(2,1)} %copy-done.12, bf16[8,258]{1,0:T(8,128)(2,1)} %copy-done.11, s32[9,4096]{1,0:T(8,128)} %n3_ref.1, ...), custom_call_target="tpu_custom_call" | custom-call | tf_op jit(solution)/shard_map/kf/pallas_call | solution.py:107
  90.8 13.2 %all-to-all-start.1 = ((bf16[128,8,512]{2,1,0:T(8,128)(2,1)}), bf16[128,8,512]{2,1,0:T(8,128)(2,1)S(1)}, u32[]{:S(2)}, u32[]{:S(2)}) async-start(bf16[128,8,512]{2,1,0:T(8,128)(2,1)} %bitcast.40), calls=%async_computation.1 | async-start | bytes 2097152 | tf_op jit(solution)/shard_map/all_to_all | solution.py:337
  104.0 21.5 %prep.2 = (s32[16,1,4096]{2,1,0:T(1,128)}, s32[512,256]{1,0:T(8,128)}, s32[16,1,256]{2,1,0:T(1,128)}) custom-call(s32[4,16384]{1,0:T(4,128)} %slot_ref.2), custom_call_target="tpu_custom_call" | custom-call | flops 25600000000 | bytes 960000 | tf_op jit(solution)/shard_map/prep/pallas_call | solution.py:208
  125.6 1.3 copy.60
  126.9 0.9 copy-done.1
  127.8 85.3 %k4.1 = (bf16[8,16384]{1,0:T(8,128)(2,1)}, bf16[1024,512]{1,0:T(8,128)(2,1)}) custom-call(s32[16,256]{1,0:T(8,128)} %bitcast.53, bf16[1024,512]{1,0:T(8,128)(2,1)} %bitcast.36, bf16[8,16384]{1,0:T(8,128)(2,1)} %tgt_ref.1, f32[4,16384]{1,0:T(4,128)} %w_ref.3, s32[16,1,4096]{2,1,0:T(1,128)} %get-tuple-element.24.pos_ref, s32[512,256]{1,0:T(8,128)} %get-tuple-element.25.code_ref), custom_call_target="tpu_custom_call" | custom-call | tf_op jit(solution)/shard_map/k4/pallas_call | solution.py:279
  213.1 9.8 %all-to-all-start.2 = ((bf16[128,8,512]{2,1,0:T(8,128)(2,1)}), bf16[128,8,512]{2,1,0:T(8,128)(2,1)S(1)}, u32[]{:S(2)}, u32[]{:S(2)}) async-start(bf16[128,8,512]{2,1,0:T(8,128)(2,1)} %bitcast.41), calls=%async_computation.2 | async-start | bytes 2097152 | tf_op jit(solution)/shard_map/all_to_all | solution.py:339
  222.9 0.7 copy.45
  224.3 17.8 %all-to-all-done.2 = bf16[128,8,512]{2,1,0:T(8,128)(2,1)S(1)} async-done(((bf16[128,8,512]{2,1,0:T(8,128)(2,1)}), bf16[128,8,512]{2,1,0:T(8,128)(2,1)S(1)}, u32[]{:S(2)}, u32[]{:S(2)}) %all-to-all-start.2) | async-done | bytes 1048608 | tf_op jit(solution)/shard_map/all_to_all | solution.py:339
  242.1 1.0 copy-done
  243.1 24.3 %kb.1 = (f32[64,72]{1,0:T(8,128)}, f32[256,64]{1,0:T(8,128)}, f32[64,256]{1,0:T(8,128)}, f32[8,64]{1,0:T(8,128)}) custom-call(bf16[1024,512]{1,0:T(8,128)(2,1)} %bitcast.35, s32[128,512]{1,0:T(8,128)} %bitcast.43, bf16[72,4096]{1,0:T(8,128)(2,1)} %get-tuple-element.28.st_ref, bf16[64,72]{1,0:T(8,128)(2,1)} %copy.43.cw_ref, bf16[256,64]{1,0:T(8,128)(2,1)} %copy.44.uw_ref, ...), custom_call_target="tpu_custom_call" | custom-call | tf_op jit(solution)/shard_map/kb/pallas_call | solution.py:166
  267.5 0.9 copy.55
  270.3 14.8 %all_to_all.49 = f32[128,1,296]{2,1,0:T(1,128)S(1)} all-to-all(f32[128,1,296]{2,1,0:T(1,128)S(1)} %all_to_all.43), channel_id=1, replica_groups=mesh['cells'=128] {'cells'}, dimensions={0} | all-to-all | bytes 303104 | tf_op jit(solution)/shard_map/all_to_all | solution.py:342
  285.3 14.6 %all_to_all.50 = f32[128,1,296]{2,1,0:T(1,128)S(1)} all-to-all(f32[128,1,296]{2,1,0:T(1,128)S(1)} %broadcast_in_dim.2), channel_id=1, replica_groups=mesh['cells'=128] {'cells'}, dimensions={0} | all-to-all | bytes 303104 | tf_op jit(solution)/shard_map/all_to_all | solution.py:343
  302.1 0.7 copy.51
  302.8 0.7 copy.52
  (57 shorter events, 8.0 us)
Async XLA Ops:
  22.9 30.7 %all-to-all-start = ((bf16[128,8,512]{2,1,0:T(8,128)(2,1)}), bf16[128,8,512]{2,1,0:T(8,128)(2,1)S(1)}, u32[]{:S(2)}, u32[]{:S(2)}) async-start(bf16[128,8,512]{2,1,0:T(8,128)(2,1)} %bitcast.38), calls=%async_computation | async-start | bytes 2097152 | tf_op jit(solution)/shard_map/all_to_all | solution.py:321
  53.6 1.0 copy-start.2
  63.7 2.1 collective-permute-start
  65.7 3.0 %collective-permute-start.1 = (bf16[8,16]{1,0:T(8,128)(2,1)S(1)}, bf16[8,16]{1,0:T(8,128)(2,1)S(1)}, u32[]{:S(2)}, u32[]{:S(2)}) collective-permute-start(bf16[8,16]{1,0:T(8,128)(2,1)S(1)} %bitcast.57), channel_id=1, source_target_pairs={{0,127},{1,0},{2,1},{3,2},{4,3},{5,4},{6,5},{7,6},{8,7},{9,8},{10,... | collective-permute-start | bytes 776 | tf_op jit(solution)/shard_map/ppermute | solution.py:307
  65.8 0.6 copy-start.8
  68.7 0.6 copy-start.9
  69.3 3.1 %copy-start.10 = (bf16[64,72]{1,0:T(8,128)(2,1)S(1)}, bf16[64,72]{1,0:T(8,128)(2,1)}, u32[]{:S(2)}) copy-start(bf16[64,72]{1,0:T(8,128)(2,1)} %param.19) | copy-start | bytes 27652
  69.4 4.7 %collective-permute-start.3 = (bf16[8,258]{1,0:T(8,128)(2,1)S(1)}, bf16[8,258]{1,0:T(8,128)(2,1)S(1)}, u32[]{:S(2)}, u32[]{:S(2)}) collective-permute-start(bf16[8,258]{1,0:T(8,128)(2,1)S(1)} %pad_maximum_fusion.2), channel_id=1, source_target_pairs={{0,112},{1,113},{2,114},{3,115},{4,116},{5,117},{6,118},{7,119},{8... | collective-permute-start | bytes 12392 | tf_op jit(solution)/shard_map/ppermute | solution.py:307
  70.2 6.1 %collective-permute-start.2 = (bf16[8,258]{1,0:T(8,128)(2,1)S(1)}, bf16[8,258]{1,0:T(8,128)(2,1)S(1)}, u32[]{:S(2)}, u32[]{:S(2)}) collective-permute-start(bf16[8,258]{1,0:T(8,128)(2,1)S(1)} %pad_maximum_fusion.1), channel_id=1, source_target_pairs={{0,16},{1,17},{2,18},{3,19},{4,20},{5,21},{6,22},{7,23},{8,24},{9,... | collective-permute-start | bytes 12392 | tf_op jit(solution)/shard_map/ppermute | solution.py:307
  72.6 0.8 copy-start.4
  74.1 2.2 copy-start.11
  76.3 0.6 copy-start.12
  90.8 36.1 %all-to-all-start.1 = ((bf16[128,8,512]{2,1,0:T(8,128)(2,1)}), bf16[128,8,512]{2,1,0:T(8,128)(2,1)S(1)}, u32[]{:S(2)}, u32[]{:S(2)}) async-start(bf16[128,8,512]{2,1,0:T(8,128)(2,1)} %bitcast.40), calls=%async_computation.1 | async-start | bytes 2097152 | tf_op jit(solution)/shard_map/all_to_all | solution.py:337
  126.9 0.9 copy-start.1
  213.1 9.8 %copy-start.3 = (bf16[64,256]{1,0:T(8,128)(2,1)S(1)}, bf16[64,256]{1,0:T(8,128)(2,1)}, u32[]{:S(2)}) copy-start(bf16[64,256]{1,0:T(8,128)(2,1)} %dw_ref.3) | copy-start | bytes 98308
  213.1 29.0 %all-to-all-start.2 = ((bf16[128,8,512]{2,1,0:T(8,128)(2,1)}), bf16[128,8,512]{2,1,0:T(8,128)(2,1)S(1)}, u32[]{:S(2)}, u32[]{:S(2)}) async-start(bf16[128,8,512]{2,1,0:T(8,128)(2,1)} %bitcast.41), calls=%async_computation.2 | async-start | bytes 2097152 | tf_op jit(solution)/shard_map/all_to_all | solution.py:339
  222.9 0.7 copy-start.7
  242.1 1.0 copy-start
  267.5 0.9 copy-start.5
  268.4 0.8 copy-start.6
  269.2 0.7 copy-start.13

commit v4 on v3

--- a/solution.py
+++ b/solution.py
@@ -174,132 +174,176 @@
 def prep_body(slot_ref, pos_ref, code_ref, gid_ref, ohp_ref):
     idx = jnp.concatenate([slot_ref[t:t+1, :] for t in range(4)], axis=1)
     d = idx >> 9
-    g = d >> 4
-    it8 = lax.broadcasted_iota(I32, (8, 256), 0)
-    hot = [jnp.where(it8 == g[:, 256*b:256*b+256], 1.0, 0.0) for b in range(16)]
+    g = (d * 147) >> 11
+    it = lax.broadcasted_iota(I32, (16, 256), 0)
+    hot = [jnp.where(it == g[:, 256*b:256*b+256], 1.0, 0.0) for b in range(16)]
     a = jnp.concatenate(hot, axis=0).astype(BF)
     sq = lambda f, n: jnp.where(f(lax.broadcasted_iota(I32, (n, n), 0), lax.broadcasted_iota(I32, (n, n), 1)), 1.0, 0.0).astype(BF)
     excl = jnp.dot(a, sq(lambda r, c: r < c, 256), preferred_element_type=F32)
     tot = jnp.dot(a, jnp.ones((256, 256), BF), preferred_element_type=F32)
-    prefix = jnp.dot(sq(lambda r, c: ((r & 7) == (c & 7)) & (c < (r & ~7)), 128), tot.astype(BF), preferred_element_type=F32)
-    count = prefix[120:128] + tot[120:128]
+    prefix = jnp.dot(sq(lambda r, c: ((r & 15) == (c & 15)) & (c < (r & ~15)), 256), tot.astype(BF), preferred_element_type=F32)
+    count = prefix[240:256] + tot[240:256]
     nblk = ((count.astype(I32) + 255) >> 8).astype(F32)
-    both = jnp.concatenate([nblk, jnp.zeros_like(nblk)], axis=0).astype(BF)
-    base = jnp.dot(sq(lambda r, c: c < r, 16), both, preferred_element_type=F32)[:8]
-    lane = lax.broadcasted_iota(I32, (8, 256), 1).astype(F32)
-    gid = jnp.sum(jnp.where(lane >= base + nblk, 1.0, 0.0), axis=0, keepdims=True).astype(I32)
-    gid_ref[0] = jnp.minimum(gid, 7)
+    base = jnp.dot(sq(lambda r, c: c < r, 16), nblk.astype(BF), preferred_element_type=F32)
+    lane = lax.broadcasted_iota(I32, (16, 256), 1)
+    gid = jnp.sum(jnp.where(lane.astype(F32) >= base + nblk, 1.0, 0.0), axis=0, keepdims=True).astype(I32)
+    used = jnp.sum(nblk, axis=0, keepdims=True).astype(I32)
+    gid_ref[0] = jnp.where(lane[:1] == 255, used, jnp.minimum(gid, GROUPS - 1))
     first = 256.0 * base
     pos = jnp.concatenate([
-        jnp.sum(hot[b] * (excl[8*b:8*b+8] + prefix[8*b:8*b+8] + first), axis=0, keepdims=True) for b in range(16)
+        jnp.sum(hot[b] * (excl[16*b:16*b+16] + prefix[16*b:16*b+16] + first), axis=0, keepdims=True) for b in range(16)
     ], axis=1).astype(I32)
     pos_ref[0] = pos
     ohp_ref[...] = onehot(pos & 255, 256)
     z = jnp.zeros((), BF)
     q = jnp.broadcast_to((pos >> 8).astype(I16), (16, 4096)) - lax.broadcasted_iota(I16, (16, 4096), 0)
-    low = jnp.broadcast_to((idx & 255).astype(F32), (16, 4096)).astype(BF)
-    high = jnp.broadcast_to(((idx >> 8) & 31).astype(F32), (16, 4096)).astype(BF)
+    code = (idx & 511) + ((d - SPAN * g) << 9)
+    low = jnp.broadcast_to((code & 255).astype(F32), (16, 4096)).astype(BF)
+    high = jnp.broadcast_to((code >> 8).astype(F32), (16, 4096)).astype(BF)
     e = jnp.concatenate([jnp.where(q == jnp.int16(16*k), v, z) for v in (low, high) for k in range(2)], axis=0)
     r = nt(e, ohp_ref[...])
     code_ref[...] = (r[:32] + 256.0 * r[32:]).astype(I32)
 
-def prep(slot):
-    n = slot.shape[1] // 1024
+def prep(slot, start, n):
     return pl.pallas_call(prep_body, grid=(n,),
-        in_specs=[pl.BlockSpec((4,1024), lambda i:(0,i))],
+        in_specs=[pl.BlockSpec((4,1024), lambda i:(0,i+start))],
         out_specs=[pl.BlockSpec((1,1,4096), lambda i:(i,0,0)), pl.BlockSpec((32,256), lambda i:(i,0)), pl.BlockSpec((1,1,256), lambda i:(i,0,0))],
         out_shape=[jax.ShapeDtypeStruct((n,1,4096), I32), jax.ShapeDtypeStruct((32*n,256), I32), jax.ShapeDtypeStruct((n,1,256), I32)],
         scratch_shapes=[pltpu.VMEM((256,4096), BF)], name="prep",
         cost_estimate=pl.CostEstimate(flops=n*1600000000, bytes_accessed=n*60000, transcendentals=0),
     )(slot)
 
-def tree24(mm, blk):
-    l8 = jnp.broadcast_to(blk, (8, blk.shape[1]))
-    m = {c: (l8 & c) != 0 for c in (1, 2, 4, 8, 16)}
+def tree_pick(mm, lo, count):
+    l8 = jnp.broadcast_to(lo, (8, lo.shape[1]))
+    top = 1
+    while top < count: top *= 2
+    m = {}
+    h = top // 2
+    while h:
+        m[h] = (l8 & h) != 0
+        h //= 2
     def tree(base, n):
         if n == 1: return mm[8*base:8*base+8]
         h = n // 2
-        return jnp.where(m[h], tree(base+h, h), tree(base, h)) if n < 32 else jnp.where(m[16], tree(16, 8), tree(0, 16))
-    return tree(0, 32)
-
-def look_up(i, tab_ref, code_ref, gid_ref, res_ref, oh_ref):
-    for b in range(0, NB, 2):
-        outs = []
-        for u in range(2):
-            code = code_ref[b+u:b+u+1, :]
-            oh = onehot(code & 511, 512)
-            if oh_ref is not None:
-                oh_ref[:, 256*(b+u):256*(b+u+1)] = oh
-            rows = tab_ref[pl.ds(pl.multiple_of(gid_ref[i, b+u] * 128, 128), 128), :]
-            mm = jnp.dot(rows, oh, preferred_element_type=F32)
-            outs.append(picktree(mm, code >> 9, 16))
-        res_ref[8*b:8*b+16, :] = jnp.concatenate(outs, axis=0).astype(BF)
-
-def blend(pos_ref, w_ref, res_ref, ohp_ref, n):
+        if base + h >= count: return tree(base, h)
+        return jnp.where(m[h], tree(base+h, h), tree(base, h))
+    return tree(0, top)
+
+def load_table(tab_ref, nat_ref):
+    nat_ref[:1024] = tab_ref[...]
+    nat_ref[1024:] = jnp.zeros((8*SPAN*GROUPS-1024, 512), BF)
+
+def look_up(i, nb, nat_ref, code_ref, gid_ref, res_ref, oh_ref):
+    half = nb // 2
+    def go(j, c):
+        for h in range(0, half, 2):
+            outs = []
+            for u in range(2):
+                b = j*half + h + u
+                code = code_ref[pl.ds(b, 1), :]
+                oh = onehot(code & 511, 512)
+                if oh_ref is not None: oh_ref[b] = oh
+                at = pl.ds(pl.multiple_of(gid_ref[i, b] * (8*SPAN), 16), 8*SPAN)
+                outs.append(tree_pick(jnp.dot(nat_ref[at, :], oh, preferred_element_type=F32), code >> 9, SPAN))
+            res_ref[pl.ds(pl.multiple_of(8*(j*half+h), 16), 16), :] = jnp.concatenate(outs, axis=0).astype(BF)
+        return c
+    lax.fori_loop(0, 2, go, 0)
+
+def blend(nb, pos_ref, w_ref, res_ref, ohp_ref, n):
     p = jnp.zeros((8, n), F32)
     for t in range(4):
         pos = pos_ref[0, :, t*n:(t+1)*n]
         ohp = onehot(pos & 255, 256)
         if ohp_ref is not None:
             ohp_ref[:, t*n:(t+1)*n] = ohp
-        mm = jnp.dot(res_ref[...], ohp, preferred_element_type=F32)
-        p = p + w_ref[t:t+1, :] * tree24(mm, pos >> 8)
+        mm = jnp.dot(res_ref[:8*nb, :], ohp, preferred_element_type=F32)
+        p = p + w_ref[t:t+1, :] * tree_pick(mm, pos >> 8, nb)
     return p
 
-def k4s_body(gid_ref, tab_ref, tgt_ref, w_ref, pos_ref, code_ref, pred_ref, send_ref, res_ref, oh_ref, ohp_ref, acc_ref):
+def k4_body(gid_ref, tab_ref, tgt_ref, w_ref, pos_ref, code_ref, pred_ref, send_ref,
+            res_ref, oh_ref, ohp_ref, sv_ref, nat_ref, acc0_ref, acc1_ref):
     i = pl.program_id(0)
     n = 1024
     scale = 1.0 / math.sqrt(2097152)
     @pl.when(i == 0)
-    def _(): acc_ref[...] = jnp.zeros_like(acc_ref)
-    look_up(i, tab_ref, code_ref, gid_ref, res_ref, oh_ref)
-    pb = blend(pos_ref, w_ref, res_ref, ohp_ref, n).astype(BF)
-    pred_ref[...] = pb
-    g = (pb.astype(F32) - tgt_ref[...].astype(F32)) * scale
-    z = jnp.zeros((), BF)
-    val = jnp.concatenate([(w_ref[t:t+1, :] * g).astype(BF) for t in range(4)], axis=1)
-    val2 = jnp.concatenate([val, val], axis=0)
-    half = lax.broadcasted_iota(I16, (16, 4*n), 0) >> 3
-    q = jnp.broadcast_to((pos_ref[0] >> 8).astype(I16), (16, 4*n)) - half
-    e = jnp.concatenate([jnp.where(q == jnp.int16(2*k), val2, z) for k in range(NB//2)], axis=0)
-    sv = nt(e, ohp_ref[...]).astype(BF)
-    half = lax.broadcasted_iota(I16, (16, 256), 0) >> 3
-    for b in range(NB):
-        vb = sv[8*b:8*b+8]
-        v2 = jnp.concatenate([vb, vb], axis=0)
-        q = jnp.broadcast_to((code_ref[b:b+1, :] >> 9).astype(I16), (16, 256)) - half
-        eb = jnp.concatenate([jnp.where(q == jnp.int16(2*k), v2, z) for k in range(8)], axis=0)
-        at = pl.ds(pl.multiple_of(gid_ref[i, b] * 128, 128), 128)
-        acc_ref[at, :] += nt(eb, oh_ref[:, 256*b:256*b+256])
+    def _():
+        load_table(tab_ref, nat_ref)
+        acc0_ref[...] = jnp.zeros_like(acc0_ref)
+        acc1_ref[...] = jnp.zeros_like(acc1_ref)
+    def run(nb):
+        look_up(i, nb, nat_ref, code_ref, gid_ref, res_ref, oh_ref)
+        pb = blend(nb, pos_ref, w_ref, res_ref, ohp_ref, n).astype(BF)
+        pred_ref[...] = pb
+        g = (pb.astype(F32) - tgt_ref[...].astype(F32)) * scale
+        z = jnp.zeros((), BF)
+        val = jnp.concatenate([(w_ref[t:t+1, :] * g).astype(BF) for t in range(4)], axis=1)
+        val2 = jnp.concatenate([val, val], axis=0)
+        row = lax.broadcasted_iota(I16, (16, 4*n), 0) >> 3
+        q = jnp.broadcast_to((pos_ref[0] >> 8).astype(I16), (16, 4*n)) - row
+        e = jnp.concatenate([jnp.where(q == jnp.int16(2*k), val2, z) for k in range(nb//2)], axis=0)
+        sv_ref[:8*nb, :] = nt(e, ohp_ref[...]).astype(BF)
+        row = lax.broadcasted_iota(I16, (16, 256), 0) >> 3
+        half = nb // 2
+        def back(j, c):
+            for h in range(0, half, 2):
+                pair = sv_ref[pl.ds(pl.multiple_of(8*(j*half+h), 16), 16), :]
+                for u, acc_ref in enumerate((acc0_ref, acc1_ref)):
+                    b = j*half + h + u
+                    vb = pair[8*u:8*u+8]
+                    v2 = jnp.concatenate([vb, vb], axis=0)
+                    q = jnp.broadcast_to((code_ref[pl.ds(b, 1), :] >> 9).astype(I16), (16, 256)) - row
+                    eb = jnp.concatenate([jnp.where(q == jnp.int16(2*k), v2, z) for k in range(SPAN//2)], axis=0)
+                    at = pl.ds(pl.multiple_of(gid_ref[i, b] * (8*SPAN), 16), 8*SPAN)
+                    acc_ref[at, :] += nt(eb, oh_ref[b])
+            return c
+        lax.fori_loop(0, 2, back, 0)
+    used = gid_ref[i, 255]
+    @pl.when(used <= FEW)
+    def _(): run(FEW)
+    @pl.when(used > FEW)
+    def _(): run(MANY)
     @pl.when(i == pl.num_programs(0)-1)
-    def _(): send_ref[...] = acc_ref[...].astype(BF)
-
-def k4s_main(tab, target, w, pos, code, gid):
+    def _(): send_ref[...] = (acc0_ref[:1024] + acc1_ref[:1024]).astype(BF)
+
+def k4(tab, target, w, pos, code, gid):
     points = target.shape[1]
-    return pl.pallas_call(k4s_body, grid=(points//1024,),
+    rows = 8*SPAN*GROUPS
+    return pl.pallas_call(k4_body, grid=(points//1024,),
         in_specs=[pl.BlockSpec(memory_space=pltpu.SMEM), pl.BlockSpec((1024,512), lambda i:(0,0)), pl.BlockSpec((8,1024), lambda i:(0,i)),
                   pl.BlockSpec((4,1024), lambda i:(0,i)), pl.BlockSpec((1,1,4096), lambda i:(i,0,0)), pl.BlockSpec((32,256), lambda i:(i,0))],
         out_specs=[pl.BlockSpec((8,1024), lambda i:(0,i)), pl.BlockSpec((1024,512), lambda i:(0,0))],
         out_shape=[jax.ShapeDtypeStruct((8,points), BF), jax.ShapeDtypeStruct((1024,512), BF)],
-        scratch_shapes=[pltpu.VMEM((8*NB,256), BF), pltpu.VMEM((512,256*NB), BF), pltpu.VMEM((256,4096), BF), pltpu.VMEM((1024,512), F32)],
+        scratch_shapes=[pltpu.VMEM((8*MANY,256), BF), pltpu.VMEM((MANY,512,256), BF), pltpu.VMEM((256,4096), BF), pltpu.VMEM((8*MANY,256), BF),
+                        pltpu.VMEM((rows,512), BF), pltpu.VMEM((rows,512), F32), pltpu.VMEM((rows,512), F32)],
         name="k4", compiler_params=pltpu.CompilerParams(vmem_limit_bytes=60*2**20),
     )(gid.reshape(-1, 256), tab, target, w, pos, code)
 
-def k2s_body(gid_ref, tab_ref, w_ref, pos_ref, code_ref, out_ref, res_ref):
-    look_up(pl.program_id(0), tab_ref, code_ref, gid_ref, res_ref, None)
-    out_ref[...] = blend(pos_ref, w_ref, res_ref, None, 1024).astype(BF)
-
-def k2s_main(tab, w, pos, code, gid):
-    return pl.pallas_call(k2s_body, grid=(4,),
+def k2_body(gid_ref, tab_ref, w_ref, pos_ref, code_ref, out_ref, res_ref, nat_ref):
+    i = pl.program_id(0)
+    @pl.when(i == 0)
+    def _(): load_table(tab_ref, nat_ref)
+    def run(nb):
+        look_up(i, nb, nat_ref, code_ref, gid_ref, res_ref, None)
+        out_ref[...] = blend(nb, pos_ref, w_ref, res_ref, None, 1024).astype(BF)
+    used = gid_ref[i, 255]
+    @pl.when(used <= FEW)
+    def _(): run(FEW)
+    @pl.when(used > FEW)
+    def _(): run(MANY)
+
+def k2(tab, w, pos, code, gid):
+    return pl.pallas_call(k2_body, grid=(4,),
         in_specs=[pl.BlockSpec(memory_space=pltpu.SMEM), pl.BlockSpec((1024,512), lambda i:(0,0)), pl.BlockSpec((4,1024), lambda i:(0,i)),
                   pl.BlockSpec((1,1,4096), lambda i:(i,0,0)), pl.BlockSpec((32,256), lambda i:(i,0))],
         out_specs=pl.BlockSpec((8,1024), lambda i:(0,i)),
         out_shape=jax.ShapeDtypeStruct((8,4096), BF),
-        scratch_shapes=[pltpu.VMEM((8*NB,256), BF)], name="k2",
+        scratch_shapes=[pltpu.VMEM((8*MANY,256), BF), pltpu.VMEM((8*SPAN*GROUPS,512), BF)], name="k2",
     )(gid.reshape(-1, 256), tab, w, pos, code)
 
 
-NB = 24
+SPAN = 14
+GROUPS = 10
+FEW, MANY = 20, 28
 
 
 def from_behind(value, by):
@@ -316,10 +360,11 @@
     exchange = functools.partial(
         lax.all_to_all, axis_name="cells", split_axis=0, concat_axis=0, tiled=True
     )
-    in_plan = prep(in_slot)
-    out_plan = prep(out_slot)
+    in_plan = prep(in_slot, 0, 4)
+    head_plan = prep(out_slot, 0, 7)
     received = exchange(k1c(ll_fields, in_rows[0]))
-    flat_reg = k2s_main(received, in_weight, *in_plan)
+    received, head_plan = lax.optimization_barrier((received, head_plan))
+    flat_reg = k2(received, in_weight, *in_plan)
     regridded = flat_reg.reshape(VARS, TILE_ROWS, TILE_WIDTH)
     left_col = from_behind(regridded[:, :, TILE_WIDTH - 1], 1)
     right_col = from_behind(regridded[:, :, 0], -1)
@@ -335,7 +380,9 @@
         down_weight, head_weight, out_rows[0],
     )
     arrived = exchange(sending)
-    predicted, slot_grad = k4s_main(arrived, target, out_weight, *out_plan)
+    tail_plan = prep(out_slot, 7, 9)
+    out_plan = [jnp.concatenate(pair, axis=0) for pair in zip(head_plan, tail_plan)]
+    predicted, slot_grad = k4(arrived, target, out_weight, *out_plan)
     returned = exchange(slot_grad)
     terms = kb(returned, out_rows[0], stacked, conv_w, up_weight, down_weight, head_weight)
     flat = jnp.concatenate([term.reshape(-1) for term in terms]).reshape(devices, -1)

time: 306 us -> 293 us (0.958)
  waiting for transfers between devices: 34 us -> 25.2 us
  Pallas kernels: 182 us -> 177 us
  other arithmetic: 0.8 us -> 3.95 us
    all_to_all x1, waiting for transfers between devices: 11.6 us -> 0.01 us  [body(): received = exchange(k1c(ll_fields, in_rows[0]))]
    pallas_call x2, Pallas kernels: 93.3 us -> 82.6 us  [the longest x1 74.1 us: k4(): pl.pallas_call(k4_body, grid=(points // 1024,), in_specs=[pl.BlockSpec(me...]
    pallas_call x2 -> x3, Pallas kernels: 27.9 us -> 33.7 us  [prep(): pl.pallas_call(prep_body, grid=(n,), in_specs=[pl.BlockSpec((4, 1024), la...]
    all_to_all x1, starting transfers between devices: 13.2 us -> 8.24 us  [body(): arrived = exchange(sending)]
    ppermute x4, starting transfers between devices: 4.23 us -> 7.33 us  [from_behind(): lax.ppermute(value, 'cells', [(i, (i + by) % devices) for i in range(devi...]
    unnamed x37 -> x44, local copies, waits for them, and re-layouts: 13.1 us -> 11.7 us
  transfers between devices with their start and end apart: 7 -> 7, of which waited for: 4 -> 4; matrix products, arithmetic and copies ran while one was open for 2% -> 3% of each run, Pallas kernels for 9% -> 12%
where the time goes in v4:
time: 293 us; the launch traced here: 291 us
  Pallas kernels  177 us (60%)
  starting transfers between devices  36.8 us (13%)
  blocking collectives  29.4 us (10%)
  waiting for transfers between devices  25.2 us (9%)
  local copies, waits for them, and re-layouts  18.1 us (6%)
  other arithmetic  3.95 us (1%)
    pallas_call x1, Pallas kernels, k4(): pl.pallas_call(k4_body, grid=(points // 1024,), in_specs=[pl.BlockSpec(me...  74.1 us
    pallas_call x3, Pallas kernels, prep(): pl.pallas_call(prep_body, grid=(n,), in_specs=[pl.BlockSpec((4, 1024), la...  33.7 us
    pallas_call x1, Pallas kernels, kb(): pl.pallas_call(kb_body, grid=(16,), in_specs=[pl.BlockSpec((64, 512), lam...  24.3 us
    pallas_call x1, Pallas kernels, k1c(): pl.pallas_call(k1c_body, grid=(16,), in_specs=[pl.BlockSpec((8, 16384), l...  22.2 us
    all_to_all x1, waiting for transfers between devices, body(): returned = exchange(slot_grad)  17.8 us
    all_to_all x1, blocking collectives, body(): part = jnp.sum(exchange(flat), axis=0, keepdims=True)  14.8 us
    all_to_all x1, blocking collectives, body(): whole = exchange(jnp.broadcast_to(part, flat.shape)).reshape(-1)  14.6 us
    pallas_call x1, Pallas kernels, kf(): pl.pallas_call(kf_body, grid=(8,), in_specs=[fix((8, 4096)), fix((8, 16))...  13.9 us
  transfers between devices with their start and end apart: 7, of which 4 were waited for; matrix products, arithmetic and copies ran while one was open for 3% of the time, Pallas kernels for 12%

profile of v4, /device:TPU:1, one launch (start us, length us, event | category | flops | bytes accessed | tf_op | source)
XLA Modules:
  0.0 291.1 jit_solution(5842666813366254811)
XLA Ops:
  0.6 22.2 %k1.1 = bf16[1024,512]{1,0:T(8,128)(2,1)} custom-call(bf16[8,16384]{1,0:T(8,128)(2,1)} %ll_ref.1, s32[128,512]{1,0:T(8,128)} %bitcast.47), custom_call_target="tpu_custom_call" | custom-call | tf_op jit(solution)/shard_map/k1/pallas_call | solution.py:54
  22.9 11.5 %all-to-all-start = ((bf16[128,8,512]{2,1,0:T(8,128)(2,1)}), bf16[128,8,512]{2,1,0:T(8,128)(2,1)S(1)}, u32[]{:S(2)}, u32[]{:S(2)}) async-start(bf16[128,8,512]{2,1,0:T(8,128)(2,1)} %bitcast.37), calls=%async_computation | async-start | bytes 2097152 | tf_op jit(solution)/shard_map/all_to_all | solution.py:365
  34.4 7.3 %prep.5 = (s32[4,1,4096]{2,1,0:T(1,128)}, s32[128,256]{1,0:T(8,128)}, s32[4,1,256]{2,1,0:T(1,128)}) custom-call(s32[4,4096]{1,0:T(4,128)} %slot_ref.5), custom_call_target="tpu_custom_call" | custom-call | flops 6400000000 | bytes 240000 | tf_op jit(solution)/shard_map/prep/pallas_call | solution.py:208
  41.6 1.3 copy.64
  42.9 11.7 %prep.3 = (s32[7,1,4096]{2,1,0:T(1,128)}, s32[224,256]{1,0:T(8,128)}, s32[7,1,256]{2,1,0:T(1,128)}) custom-call(s32[4,16384]{1,0:T(4,128)} %slot_ref.4), custom_call_target="tpu_custom_call" | custom-call | flops 11200000000 | bytes 420000 | tf_op jit(solution)/shard_map/prep/pallas_call | solution.py:208
  54.6 1.0 copy-done.2
  55.6 8.5 %k2.1.reg_ref = bf16[8,4096]{1,0:T(8,128)(2,1)} custom-call(s32[4,256]{1,0:T(4,128)} %bitcast.53, bf16[1024,512]{1,0:T(8,128)(2,1)} %bitcast.36, f32[4,4096]{1,0:T(4,128)} %w_ref.2, s32[4,1,4096]{2,1,0:T(1,128)} %get-tuple-element.33.pos_ref, s32[128,256]{1,0:T(8,128)} %get-tuple-element.34.code_ref), custom_call_target="tpu_custom_call" | custom-call | tf_op jit(solution)/shard_map/k2/pallas_call | solution.py:335
  64.1 0.9 fusion
  65.1 1.6 collective-permute-start
  66.7 0.7 slice_bitcast_fusion
  68.2 2.4 collective-permute-done.1.rc_ref
  71.3 5.6 %collective-permute-start.3 = (bf16[8,258]{1,0:T(8,128)(2,1)S(1)}, bf16[8,258]{1,0:T(8,128)(2,1)S(1)}, u32[]{:S(2)}, u32[]{:S(2)}) collective-permute-start(bf16[8,258]{1,0:T(8,128)(2,1)S(1)} %pad_maximum_fusion.2), channel_id=1, source_target_pairs={{0,112},{1,113},{2,114},{3,115},{4,116},{5,117},{6,118},{7,119},{8... | collective-permute-start | bytes 12392 | tf_op jit(solution)/shard_map/ppermute | solution.py:351
  77.9 0.7 copy.50.uw_ref
  78.6 4.4 %collective-permute-done.2.up_ref = bf16[8,258]{1,0:T(8,128)(2,1)S(1)} collective-permute-done((bf16[8,258]{1,0:T(8,128)(2,1)S(1)}, bf16[8,258]{1,0:T(8,128)(2,1)S(1)}, u32[]{:S(2)}, u32[]{:S(2)}) %collective-permute-start.2) | collective-permute-done | bytes 4160 | tf_op jit(solution)/shard_map/ppermute | solution.py:351
  83.7 13.9 %kf.1 = (bf16[1024,512]{1,0:T(8,128)(2,1)}, bf16[72,4096]{1,0:T(8,128)(2,1)}) custom-call(bf16[8,4096]{1,0:T(8,128)(2,1)} %k2.1.reg_ref, bf16[8,16]{1,0:T(8,128)(2,1)} %copy-done.11, bf16[8,16]{1,0:T(8,128)(2,1)} %copy-done.12, bf16[8,258]{1,0:T(8,128)(2,1)} %copy-done.16, bf16[8,258]{1,0:T(8,128)(2,1)} %copy-done.15, s32[9,4096]{1,0:T(8,128)} %n3_ref.1, ...), custom_call_target="tpu_custom_call" | custom-call | tf_op jit(solution)/shard_map/kf/pallas_call | solution.py:107
  97.6 8.2 %all-to-all-start.1 = ((bf16[128,8,512]{2,1,0:T(8,128)(2,1)}), bf16[128,8,512]{2,1,0:T(8,128)(2,1)S(1)}, u32[]{:S(2)}, u32[]{:S(2)}) async-start(bf16[128,8,512]{2,1,0:T(8,128)(2,1)} %bitcast.39), calls=%async_computation.1 | async-start | bytes 2097152 | tf_op jit(solution)/shard_map/all_to_all | solution.py:382
  105.9 14.7 %prep.4 = (s32[9,1,4096]{2,1,0:T(1,128)}, s32[288,256]{1,0:T(8,128)}, s32[9,1,256]{2,1,0:T(1,128)}) custom-call(s32[4,16384]{1,0:T(4,128)} %slot_ref.4), custom_call_target="tpu_custom_call" | custom-call | flops 14400000000 | bytes 540000 | tf_op jit(solution)/shard_map/prep/pallas_call | solution.py:208
  120.6 0.7 copy.44
  121.9 1.8 pad_add_fusion.code_ref
  123.8 0.7 pad_add_fusion.1.pos_ref
  125.1 1.0 copy-done
  126.0 74.1 %k4.1 = (bf16[8,16384]{1,0:T(8,128)(2,1)}, bf16[1024,512]{1,0:T(8,128)(2,1)}) custom-call(s32[16,256]{1,0:T(8,128)} %add_bitcast_fusion.gid_ref, bf16[1024,512]{1,0:T(8,128)(2,1)} %bitcast.34, bf16[8,16384]{1,0:T(8,128)(2,1)} %tgt_ref.1, f32[4,16384]{1,0:T(4,128)} %w_ref.3, s32[16,1,4096]{2,1,0:T(1,128)} %pad_add_fusion.1.pos_ref, ...), custom_call_target="tpu_custom_call" | custom-call | tf_op jit(solution)/shard_map/k4/pallas_call | solution.py:311
  200.1 9.7 %all-to-all-start.2 = ((bf16[128,8,512]{2,1,0:T(8,128)(2,1)}), bf16[128,8,512]{2,1,0:T(8,128)(2,1)S(1)}, u32[]{:S(2)}, u32[]{:S(2)}) async-start(bf16[128,8,512]{2,1,0:T(8,128)(2,1)} %bitcast.40), calls=%async_computation.2 | async-start | bytes 2097152 | tf_op jit(solution)/shard_map/all_to_all | solution.py:386
  209.8 0.7 copy.51
  211.3 17.8 %all-to-all-done.2 = bf16[128,8,512]{2,1,0:T(8,128)(2,1)S(1)} async-done(((bf16[128,8,512]{2,1,0:T(8,128)(2,1)}), bf16[128,8,512]{2,1,0:T(8,128)(2,1)S(1)}, u32[]{:S(2)}, u32[]{:S(2)}) %all-to-all-start.2) | async-done | bytes 1048608 | tf_op jit(solution)/shard_map/all_to_all | solution.py:386
  229.1 1.0 copy-done.1
  230.0 24.3 %kb.1 = (f32[64,72]{1,0:T(8,128)}, f32[256,64]{1,0:T(8,128)}, f32[64,256]{1,0:T(8,128)}, f32[8,64]{1,0:T(8,128)}) custom-call(bf16[1024,512]{1,0:T(8,128)(2,1)} %bitcast.35, s32[128,512]{1,0:T(8,128)} %bitcast.42, bf16[72,4096]{1,0:T(8,128)(2,1)} %get-tuple-element.42.st_ref, bf16[64,72]{1,0:T(8,128)(2,1)} %copy.49.cw_ref, bf16[256,64]{1,0:T(8,128)(2,1)} %copy.50.uw_ref, ...), custom_call_target="tpu_custom_call" | custom-call | tf_op jit(solution)/shard_map/kb/pallas_call | solution.py:166
  254.4 0.9 copy.60
  257.2 14.8 %all_to_all.50 = f32[128,1,296]{2,1,0:T(1,128)S(1)} all-to-all(f32[128,1,296]{2,1,0:T(1,128)S(1)} %all_to_all.44), channel_id=1, replica_groups=mesh['cells'=128] {'cells'}, dimensions={0} | all-to-all | bytes 303104 | tf_op jit(solution)/shard_map/all_to_all | solution.py:389
  272.2 14.6 %all_to_all.51 = f32[128,1,296]{2,1,0:T(1,128)S(1)} all-to-all(f32[128,1,296]{2,1,0:T(1,128)S(1)} %broadcast_in_dim.2), channel_id=1, replica_groups=mesh['cells'=128] {'cells'}, dimensions={0} | all-to-all | bytes 303104 | tf_op jit(solution)/shard_map/all_to_all | solution.py:390
  289.0 0.7 copy.57
  289.7 0.7 copy.58
  (70 shorter events, 9.9 us)
Async XLA Ops:
  22.9 31.7 %all-to-all-start = ((bf16[128,8,512]{2,1,0:T(8,128)(2,1)}), bf16[128,8,512]{2,1,0:T(8,128)(2,1)S(1)}, u32[]{:S(2)}, u32[]{:S(2)}) async-start(bf16[128,8,512]{2,1,0:T(8,128)(2,1)} %bitcast.37), calls=%async_computation | async-start | bytes 2097152 | tf_op jit(solution)/shard_map/all_to_all | solution.py:365
  54.6 1.0 copy-start.2
  65.1 2.5 collective-permute-start
  67.6 3.0 %collective-permute-start.1 = (bf16[8,16]{1,0:T(8,128)(2,1)S(1)}, bf16[8,16]{1,0:T(8,128)(2,1)S(1)}, u32[]{:S(2)}, u32[]{:S(2)}) collective-permute-start(bf16[8,16]{1,0:T(8,128)(2,1)S(1)} %bitcast.55), channel_id=1, source_target_pairs={{0,127},{1,0},{2,1},{3,2},{4,3},{5,4},{6,5},{7,6},{8,7},{9,8},{10,... | collective-permute-start | bytes 776 | tf_op jit(solution)/shard_map/ppermute | solution.py:351
  67.6 0.6 copy-start.11
  70.6 0.6 copy-start.12
  71.2 5.8 %copy-start.13 = (bf16[64,72]{1,0:T(8,128)(2,1)S(1)}, bf16[64,72]{1,0:T(8,128)(2,1)}, u32[]{:S(2)}) copy-start(bf16[64,72]{1,0:T(8,128)(2,1)} %param.19) | copy-start | bytes 27652
  71.3 7.3 %collective-permute-start.3 = (bf16[8,258]{1,0:T(8,128)(2,1)S(1)}, bf16[8,258]{1,0:T(8,128)(2,1)S(1)}, u32[]{:S(2)}, u32[]{:S(2)}) collective-permute-start(bf16[8,258]{1,0:T(8,128)(2,1)S(1)} %pad_maximum_fusion.2), channel_id=1, source_target_pairs={{0,112},{1,113},{2,114},{3,115},{4,116},{5,117},{6,118},{7,119},{8... | collective-permute-start | bytes 12392 | tf_op jit(solution)/shard_map/ppermute | solution.py:351
  77.0 6.1 %collective-permute-start.2 = (bf16[8,258]{1,0:T(8,128)(2,1)S(1)}, bf16[8,258]{1,0:T(8,128)(2,1)S(1)}, u32[]{:S(2)}, u32[]{:S(2)}) collective-permute-start(bf16[8,258]{1,0:T(8,128)(2,1)S(1)} %pad_maximum_fusion.1), channel_id=1, source_target_pairs={{0,16},{1,17},{2,18},{3,19},{4,20},{5,21},{6,22},{7,23},{8,24},{9,... | collective-permute-start | bytes 12392 | tf_op jit(solution)/shard_map/ppermute | solution.py:351
  77.1 0.8 copy-start.6
  78.6 4.5 %copy-start.15 = (bf16[8,258]{1,0:T(8,128)(2,1)}, bf16[8,258]{1,0:T(8,128)(2,1)S(1)}, u32[]{:S(2)}) copy-start(bf16[8,258]{1,0:T(8,128)(2,1)S(1)} %collective-permute-done.3.lw_ref) | copy-start | bytes 12388
  83.1 0.6 copy-start.16
  97.6 27.5 %all-to-all-start.1 = ((bf16[128,8,512]{2,1,0:T(8,128)(2,1)}), bf16[128,8,512]{2,1,0:T(8,128)(2,1)S(1)}, u32[]{:S(2)}, u32[]{:S(2)}) async-start(bf16[128,8,512]{2,1,0:T(8,128)(2,1)} %bitcast.39), calls=%async_computation.1 | async-start | bytes 2097152 | tf_op jit(solution)/shard_map/all_to_all | solution.py:382
  105.8 16.1 %copy-start.4 = (s32[224,256]{1,0:T(8,128)S(1)}, s32[224,256]{1,0:T(8,128)}, u32[]{:S(2)}) copy-start(s32[224,256]{1,0:T(8,128)} %get-tuple-element.38) | copy-start | bytes 688132
  120.6 0.7 copy-start.14
  121.9 1.8 copy-start.5
  121.9 1.8 copy-start.8
  125.1 1.0 copy-start
  200.1 9.7 %copy-start.3 = (bf16[64,256]{1,0:T(8,128)(2,1)S(1)}, bf16[64,256]{1,0:T(8,128)(2,1)}, u32[]{:S(2)}) copy-start(bf16[64,256]{1,0:T(8,128)(2,1)} %dw_ref.3) | copy-start | bytes 98308
  200.1 28.9 %all-to-all-start.2 = ((bf16[128,8,512]{2,1,0:T(8,128)(2,1)}), bf16[128,8,512]{2,1,0:T(8,128)(2,1)S(1)}, u32[]{:S(2)}, u32[]{:S(2)}) async-start(bf16[128,8,512]{2,1,0:T(8,128)(2,1)} %bitcast.40), calls=%async_computation.2 | async-start | bytes 2097152 | tf_op jit(solution)/shard_map/all_to_all | solution.py:386
  209.8 0.7 copy-start.10
  229.1 1.0 copy-start.1
  254.4 0.9 copy-start.7
  255.3 0.8 copy-start.9
  256.1 0.7 copy-start.17

commit v5 on v4

--- a/solution.py
+++ b/solution.py
@@ -56,6 +56,17 @@
         out_specs=pl.BlockSpec((64,512), lambda i:(i,0)),
         out_shape=jax.ShapeDtypeStruct((1024,512), BF),
         scratch_shapes=[pltpu.VMEM((256,512), BF)], name="k1")(ll, rows)
+
+def gelu_both(x):
+    c = math.sqrt(2 / math.pi)
+    x2 = x * x
+    th = jnp.tanh(c * (x + 0.044715 * x2 * x))
+    act = x * (0.5 * (1.0 + th))
+    der = 0.5 * (1.0 + th) + 0.5 * x * (1.0 - th * th) * (c * (1.0 + 3 * 0.044715 * x2))
+    return act, der
+
+def nt(a, b):
+    return lax.dot_general(a, b, (((1,), (1,)), ((), ())), preferred_element_type=F32)
 
 def kf_body(reg_ref, lc_ref, rc_ref, up_ref, lw_ref, n0_ref, n1_ref, n2_ref, n3_ref, cw_ref, uw_ref, dw_ref, hw_ref, rows_ref,
             out_ref, st_ref, tab_ref):
@@ -93,83 +104,112 @@
             tab_ref[pl.ds(pl.multiple_of(16*j,16),16), :] = jnp.concatenate([head[:, :256], head[:, 256:]], axis=0)
             return c
         lax.fori_loop(0, 8, chunk, 0)
-    for j in range(8):
-        outs = []
-        for u in range(2):
-            idx = rows_ref[2*j+u:2*j+u+1, :]
-            mm = jnp.dot(tab_ref[...], onehot(idx & 255, 256), preferred_element_type=F32)
-            outs.append(picktree(mm, idx >> 8, 16))
-        out_ref[16*j:16*j+16, :] = jnp.concatenate(outs, 0).astype(BF)
+    def part(k, c):
+        rows = rows_ref[pl.ds(pl.multiple_of(16*k, 16), 16), :]
+        for j in range(8):
+            outs = []
+            for u in range(2):
+                idx = rows[2*j+u:2*j+u+1]
+                mm = jnp.dot(tab_ref[...], onehot(idx & 255, 256), preferred_element_type=F32)
+                outs.append(picktree(mm, idx >> 8, 16))
+            out_ref[pl.ds(pl.multiple_of(128*k + 16*j, 16), 16), :] = jnp.concatenate(outs, 0).astype(BF)
+        return c
+    lax.fori_loop(0, 2, part, 0)
 
 def kf(reg, lc, rc, up, lw, neigh, cw, uw, dw, hw, rows):
     fix = lambda s: pl.BlockSpec(s, lambda i: (0, 0))
     nb = lambda b: pl.BlockSpec((9, 128), lambda i: (0, b))
-    return pl.pallas_call(kf_body, grid=(8,),
+    return pl.pallas_call(kf_body, grid=(4,),
         in_specs=[fix((8,4096)), fix((8,16)), fix((8,16)), fix((8,258)), fix((8,258)), nb(0), nb(1), nb(30), nb(31),
-                  fix((64,72)), fix((256,64)), fix((64,256)), fix((8,64)), pl.BlockSpec((16,512), lambda i:(i,0))],
-        out_specs=[pl.BlockSpec((128,512), lambda i:(i,0)), fix((72,4096))],
+                  fix((64,72)), fix((256,64)), fix((64,256)), fix((8,64)), pl.BlockSpec((32,512), lambda i:(i,0))],
+        out_specs=[pl.BlockSpec((256,512), lambda i:(i,0)), fix((72,4096))],
         out_shape=[jax.ShapeDtypeStruct((1024,512), BF), jax.ShapeDtypeStruct((72,4096), BF)],
         scratch_shapes=[pltpu.VMEM((128,256), BF)], name="kf",
     )(reg, lc, rc, up, lw, neigh, neigh, neigh, neigh, cw, uw, dw, hw, rows)
 
-def gelu_both(x):
-    c = math.sqrt(2 / math.pi)
-    x2 = x * x
-    th = jnp.tanh(c * (x + 0.044715 * x2 * x))
-    act = x * (0.5 * (1.0 + th))
-    der = 0.5 * (1.0 + th) + 0.5 * x * (1.0 - th * th) * (c * (1.0 + 3 * 0.044715 * x2))
-    return act, der
-
-def nt(a, b):
-    return lax.dot_general(a, b, (((1,), (1,)), ((), ())), preferred_element_type=F32)
-
-def kb_body(sg_ref, rows_ref, st_ref, cw_ref, uw_ref, dw_ref, hw_ref, ut_ref, dt_ref, ht_ref,
-            gc_ref, gu_ref, gd_ref, gh_ref, acc_ref):
+def kr_body(st_ref, cw_ref, uw_ref, dw_ref, cb_ref, act_ref, der_ref, mix_ref):
+    conv = jnp.dot(cw_ref[...], st_ref[...], preferred_element_type=F32)
+    cb = conv.astype(BF)
+    cb_ref[...] = cb
+    act, der = gelu_both(jnp.dot(uw_ref[...], cb, preferred_element_type=F32))
+    act = act.astype(BF)
+    act_ref[...] = act
+    der_ref[...] = der
+    mix_ref[...] = (conv + jnp.dot(dw_ref[...], act, preferred_element_type=F32)).astype(BF)
+
+def kr(st, cw, uw, dw):
+    fix = lambda s: pl.BlockSpec(s, lambda i: (0, 0))
+    col = lambda r: pl.BlockSpec((r, 512), lambda i: (0, i))
+    return pl.pallas_call(kr_body, grid=(8,),
+        in_specs=[col(72), fix((64,72)), fix((256,64)), fix((64,256))],
+        out_specs=[col(64), col(256), col(256), col(64)],
+        out_shape=[jax.ShapeDtypeStruct((64,4096), BF), jax.ShapeDtypeStruct((256,4096), BF), jax.ShapeDtypeStruct((256,4096), F32), jax.ShapeDtypeStruct((64,4096), BF)],
+        name="kr", cost_estimate=pl.CostEstimate(flops=10**10, bytes_accessed=8*10**6, transcendentals=10**6),
+    )(st, cw, uw, dw)
+
+def kb_body(sg_ref, rows_ref, st_ref, cb_ref, act_ref, der_ref, mix_ref, ut_ref, dt_ref, ht_ref,
+            out_ref, acc_ref, gd_ref, gu_ref, ch_ref, go_ref):
     i = pl.program_id(0)
     @pl.when(i == 0)
-    def _(): acc_ref[...] = jnp.zeros_like(acc_ref)
-    half = lax.broadcasted_iota(I16, (16, 4096), 0) >> 3
-    z = jnp.zeros((), BF)
-    val = jnp.concatenate([sg_ref[8*j:8*j+8, :] for j in range(8)], axis=1)
-    idx = jnp.concatenate([rows_ref[j:j+1, :] for j in range(8)], axis=1)
-    val2 = jnp.concatenate([val, val], axis=0)
-    q = jnp.broadcast_to((idx >> 8).astype(I16), (16, 4096)) - half
-    e = jnp.concatenate([jnp.where(q == jnp.int16(2*k), val2, z) for k in range(8)], axis=0)
-    acc_ref[...] += nt(e, onehot(idx & 255, 256))
+    def _():
+        for ref in (acc_ref, gd_ref, gu_ref, ch_ref): ref[...] = jnp.zeros_like(ref)
+    @pl.when(i < 4)
+    def _():
+        half = lax.broadcasted_iota(I16, (16, 4096), 0) >> 3
+        z = jnp.zeros((), BF)
+        def part(j, c):
+            sg = sg_ref[pl.ds(pl.multiple_of(64*j, 64), 64), :]
+            rows = rows_ref[pl.ds(pl.multiple_of(8*j, 8), 8), :]
+            val = jnp.concatenate([sg[8*k:8*k+8] for k in range(8)], axis=1)
+            idx = jnp.concatenate([rows[k:k+1] for k in range(8)], axis=1)
+            val2 = jnp.concatenate([val, val], axis=0)
+            q = jnp.broadcast_to((idx >> 8).astype(I16), (16, 4096)) - half
+            e = jnp.concatenate([jnp.where(q == jnp.int16(2*k), val2, z) for k in range(8)], axis=0)
+            hot = onehot(idx & 255, 256)
+            acc_ref[...] += sum(nt(hot[:, 1024*k:1024*k+1024], e[:, 1024*k:1024*k+1024]) for k in range(4))
+            return c
+        lax.fori_loop(0, 4, part, 0)
+        @pl.when(i == 3)
+        def _(): go_ref[...] = acc_ref[...].T
+    @pl.when(i >= 4)
+    def _():
+        a2 = go_ref[pl.ds(pl.multiple_of(16*(i-4),16),16), :]
+        go = jnp.concatenate([a2[:8], a2[8:]], axis=1).astype(BF)
+        gm = jnp.dot(ht_ref[...], go, preferred_element_type=F32)
+        gmb = gm.astype(BF)
+        ch_ref[:, 72:80] += nt(mix_ref[...], go)
+        gp = (jnp.dot(dt_ref[...], gmb, preferred_element_type=F32) * der_ref[...]).astype(BF)
+        gd_ref[...] += nt(gmb, act_ref[...])
+        gu_ref[...] += nt(cb_ref[...], gp)
+        gco = (gm + jnp.dot(ut_ref[...], gp, preferred_element_type=F32)).astype(BF)
+        ch_ref[:, :72] += nt(gco, st_ref[...])
     @pl.when(i == pl.num_programs(0)-1)
     def _():
-        gc_ref[...] = jnp.zeros_like(gc_ref); gu_ref[...] = jnp.zeros_like(gu_ref)
-        gd_ref[...] = jnp.zeros_like(gd_ref); gh_ref[...] = jnp.zeros_like(gh_ref)
-        def chunk(j, c):
-            s = st_ref[:, pl.ds(pl.multiple_of(j*512, 512), 512)]
-            a2 = acc_ref[pl.ds(pl.multiple_of(16*j,16),16), :]
-            go = jnp.concatenate([a2[:8], a2[8:]], axis=1).astype(BF)
-            conv = jnp.dot(cw_ref[...], s, preferred_element_type=F32)
-            cb = conv.astype(BF)
-            pre = jnp.dot(uw_ref[...], cb, preferred_element_type=F32)
-            act, der = gelu_both(pre)
-            act = act.astype(BF)
-            mixed = (conv + jnp.dot(dw_ref[...], act, preferred_element_type=F32)).astype(BF)
-            gm = jnp.dot(ht_ref[...], go, preferred_element_type=F32)
-            gmb = gm.astype(BF)
-            gh_ref[...] += nt(go, mixed)
-            gp = (jnp.dot(dt_ref[...], gmb, preferred_element_type=F32) * der).astype(BF)
-            gd_ref[...] += nt(gmb, act)
-            gu_ref[...] += nt(gp, cb)
-            gco = (gm + jnp.dot(ut_ref[...], gp, preferred_element_type=F32)).astype(BF)
-            gc_ref[...] += nt(gco, s)
-            return c
-        lax.fori_loop(0, 8, chunk, 0)
-
-def kb(sg, rows, st, cw, uw, dw, hw):
+        p = lax.broadcasted_iota(I32, (128, 128), 0)
+        q = lax.broadcasted_iota(I32, (128, 128), 1)
+        v = (q * 57) >> 9
+        perm = jnp.where(p == jnp.where(q < 72, (q - 9 * v) * 8 + v, q), 1.0, 0.0)
+        out_ref[0:64] = gd_ref[:, :128]
+        out_ref[64:128] = gd_ref[:, 128:]
+        out_ref[128:192] = gu_ref[:, :128]
+        out_ref[192:256] = gu_ref[:, 128:]
+        out_ref[256:320] = jnp.dot(ch_ref[...], perm, precision=lax.Precision.HIGHEST, preferred_element_type=F32)
+        out_ref[320:384] = jnp.zeros((64, 128), F32)
+
+def kb(sg, rows, st, saved, uw, dw, hw):
     fix = lambda s: pl.BlockSpec(s, lambda i: (0, 0))
-    return pl.pallas_call(kb_body, grid=(16,),
-        in_specs=[pl.BlockSpec((64,512), lambda i:(i,0)), pl.BlockSpec((8,512), lambda i:(i,0)), fix((72,4096)),
-                  fix((64,72)), fix((256,64)), fix((64,256)), fix((8,64)), fix((64,256)), fix((256,64)), fix((64,8))],
-        out_specs=[fix((64,72)), fix((256,64)), fix((64,256)), fix((8,64))],
-        out_shape=[jax.ShapeDtypeStruct(s, F32) for s in ((64,72), (256,64), (64,256), (8,64))],
-        scratch_shapes=[pltpu.VMEM((128,256), F32)], name="kb",
-    )(sg, rows, st, cw, uw, dw, hw, uw.T, dw.T, hw.T)
+    col = lambda r: pl.BlockSpec((r, 512), lambda i: (0, jnp.maximum(i - 4, 0)))
+    blk = lambda s: pl.BlockSpec(s, lambda i: (jnp.minimum(i, 3), 0))
+    return pl.pallas_call(kb_body, grid=(12,),
+        in_specs=[blk((256,512)), blk((32,512)), col(72), col(64), col(256), col(256), col(64), fix((64,256)), fix((256,64)), fix((64,8))],
+        out_specs=fix((384,128)), out_shape=jax.ShapeDtypeStruct((384,128), F32),
+        scratch_shapes=[pltpu.VMEM((256,128), F32), pltpu.VMEM((64,256), F32), pltpu.VMEM((64,256), F32), pltpu.VMEM((64,128), F32), pltpu.VMEM((128,256), F32)], name="kb",
+    )(sg, rows, st, *saved, uw.T, dw.T, hw.T)
+
+def unpack(whole):
+    down = jnp.concatenate([whole[0:64], whole[64:128]], axis=1)
+    up = jnp.concatenate([whole[128:192], whole[192:256]], axis=1).T
+    return whole[256:320, :72], up, down, whole[256:320, 72:80].T
 
 def prep_body(slot_ref, pos_ref, code_ref, gid_ref, ohp_ref):
     idx = jnp.concatenate([slot_ref[t:t+1, :] for t in range(4)], axis=1)
@@ -201,7 +241,7 @@
     low = jnp.broadcast_to((code & 255).astype(F32), (16, 4096)).astype(BF)
     high = jnp.broadcast_to((code >> 8).astype(F32), (16, 4096)).astype(BF)
     e = jnp.concatenate([jnp.where(q == jnp.int16(16*k), v, z) for v in (low, high) for k in range(2)], axis=0)
-    r = nt(e, ohp_ref[...])
+    r = nt(ohp_ref[...], e).T
     code_ref[...] = (r[:32] + 256.0 * r[32:]).astype(I32)
 
 def prep(slot, start, n):
@@ -281,7 +321,7 @@
         row = lax.broadcasted_iota(I16, (16, 4*n), 0) >> 3
         q = jnp.broadcast_to((pos_ref[0] >> 8).astype(I16), (16, 4*n)) - row
         e = jnp.concatenate([jnp.where(q == jnp.int16(2*k), val2, z) for k in range(nb//2)], axis=0)
-        sv_ref[:8*nb, :] = nt(e, ohp_ref[...]).astype(BF)
+        sv_ref[:8*nb, :] = nt(ohp_ref[...], e).T.astype(BF)
         row = lax.broadcasted_iota(I16, (16, 256), 0) >> 3
         half = nb // 2
         def back(j, c):
@@ -292,9 +332,8 @@
                     vb = pair[8*u:8*u+8]
                     v2 = jnp.concatenate([vb, vb], axis=0)
                     q = jnp.broadcast_to((code_ref[pl.ds(b, 1), :] >> 9).astype(I16), (16, 256)) - row
-                    eb = jnp.concatenate([jnp.where(q == jnp.int16(2*k), v2, z) for k in range(SPAN//2)], axis=0)
-                    at = pl.ds(pl.multiple_of(gid_ref[i, b] * (8*SPAN), 16), 8*SPAN)
-                    acc_ref[at, :] += nt(eb, oh_ref[b])
+                    eb = jnp.concatenate([jnp.where(q == jnp.int16(2*k), v2, z) for k in range(8)], axis=0)
+                    acc_ref[gid_ref[i, b]] += nt(oh_ref[b], eb)
             return c
         lax.fori_loop(0, 2, back, 0)
     used = gid_ref[i, 255]
@@ -303,7 +342,10 @@
     @pl.when(used > FEW)
     def _(): run(MANY)
     @pl.when(i == pl.num_programs(0)-1)
-    def _(): send_ref[...] = (acc0_ref[:1024] + acc1_ref[:1024]).astype(BF)
+    def _():
+        for g in range(GROUPS):
+            rows = min(8*SPAN, 1024 - 8*SPAN*g)
+            send_ref[8*SPAN*g:8*SPAN*g+rows, :] = (acc0_ref[g] + acc1_ref[g]).T[:rows].astype(BF)
 
 def k4(tab, target, w, pos, code, gid):
     points = target.shape[1]
@@ -314,7 +356,7 @@
         out_specs=[pl.BlockSpec((8,1024), lambda i:(0,i)), pl.BlockSpec((1024,512), lambda i:(0,0))],
         out_shape=[jax.ShapeDtypeStruct((8,points), BF), jax.ShapeDtypeStruct((1024,512), BF)],
         scratch_shapes=[pltpu.VMEM((8*MANY,256), BF), pltpu.VMEM((MANY,512,256), BF), pltpu.VMEM((256,4096), BF), pltpu.VMEM((8*MANY,256), BF),
-                        pltpu.VMEM((rows,512), BF), pltpu.VMEM((rows,512), F32), pltpu.VMEM((rows,512), F32)],
+                        pltpu.VMEM((rows,512), BF), pltpu.VMEM((GROUPS,512,128), F32), pltpu.VMEM((GROUPS,512,128), F32)],
         name="k4", compiler_params=pltpu.CompilerParams(vmem_limit_bytes=60*2**20),
     )(gid.reshape(-1, 256), tab, target, w, pos, code)
 
@@ -383,17 +425,14 @@
     tail_plan = prep(out_slot, 7, 9)
     out_plan = [jnp.concatenate(pair, axis=0) for pair in zip(head_plan, tail_plan)]
     predicted, slot_grad = k4(arrived, target, out_weight, *out_plan)
+    slot_grad, stacked = lax.optimization_barrier((slot_grad, stacked))
+    saved = kr(stacked, conv_w, up_weight, down_weight)
     returned = exchange(slot_grad)
-    terms = kb(returned, out_rows[0], stacked, conv_w, up_weight, down_weight, head_weight)
-    flat = jnp.concatenate([term.reshape(-1) for term in terms]).reshape(devices, -1)
+    packed = kb(returned, out_rows[0], stacked, saved, up_weight, down_weight, head_weight)
+    flat = packed.reshape(devices, -1, 128)
     part = jnp.sum(exchange(flat), axis=0, keepdims=True)
-    whole = exchange(jnp.broadcast_to(part, flat.shape)).reshape(-1)
-    totals, at = [], 0
-    for term in terms:
-        totals.append(whole[at : at + term.size].reshape(term.shape))
-        at += term.size
-    totals[0] = totals[0].reshape(64, 9, VARS).transpose(0, 2, 1).reshape(64, 72)
-    return (predicted, *totals)
+    whole = exchange(jnp.broadcast_to(part, flat.shape)).reshape(packed.shape)
+    return (predicted, *unpack(whole))
 
 
 def solution(mesh):

time: 293 us -> 286 us (0.976)
  waiting for transfers between devices: 25.2 us -> 12.2 us
  local copies, waits for them, and re-layouts: 18.1 us -> 13 us
  starting transfers between devices: 36.8 us -> 41.6 us
  Pallas kernels: 177 us -> 181 us
    all_to_all x1, waiting for transfers between devices: 17.8 us -> 9.25 us  [body(): returned = exchange(slot_grad)]
    pallas_call x2 -> x3, Pallas kernels: 38.3 us -> 44.6 us  [the longest x1 22 us: kb(): pl.pallas_call(kb_body, grid=(12,), in_specs=[blk((256, 512)), blk((32, 5...]
    unnamed x44 -> x34, local copies, waits for them, and re-layouts: 11.7 us -> 7.7 us
    ppermute x4, waiting for transfers between devices: 6.86 us -> 2.91 us  [from_behind(): lax.ppermute(value, 'cells', [(i, (i + by) % devices) for i in range(devi...]
    all_to_all x1, starting transfers between devices: 8.24 us -> 11.7 us  [body(): arrived = exchange(sending)]
    pallas_call x1, Pallas kernels: 74.1 us -> 71.1 us  [k4(): pl.pallas_call(k4_body, grid=(points // 1024,), in_specs=[pl.BlockSpec(me...]
  transfers between devices with their start and end apart: 7 -> 7, of which waited for: 4 -> 2; matrix products, arithmetic and copies ran while one was open for 3% -> 4% of each run, Pallas kernels for 12% -> 15%
where the time goes in v5:
time: 286 us; the launch traced here: 284 us
  Pallas kernels  181 us (63%)
  starting transfers between devices  41.6 us (15%)
  blocking collectives  30.7 us (11%)
  local copies, waits for them, and re-layouts  13 us (5%)
  waiting for transfers between devices  12.2 us (4%)
  other arithmetic  5.02 us (2%)
    pallas_call x1, Pallas kernels, k4(): pl.pallas_call(k4_body, grid=(points // 1024,), in_specs=[pl.BlockSpec(me...  71.1 us
    pallas_call x3, Pallas kernels, prep(): pl.pallas_call(prep_body, grid=(n,), in_specs=[pl.BlockSpec((4, 1024), la...  33.9 us
    pallas_call x1, Pallas kernels, k1c(): pl.pallas_call(k1c_body, grid=(16,), in_specs=[pl.BlockSpec((8, 16384), l...  22.2 us
    pallas_call x1, Pallas kernels, kb(): pl.pallas_call(kb_body, grid=(12,), in_specs=[blk((256, 512)), blk((32, 5...  22 us
    all_to_all x1, blocking collectives, body(): part = jnp.sum(exchange(flat), axis=0, keepdims=True)  15.4 us
    all_to_all x1, blocking collectives, body(): whole = exchange(jnp.broadcast_to(part, flat.shape)).reshape(packed.shape)  15.3 us
    pallas_call x1, Pallas kernels, kf(): pl.pallas_call(kf_body, grid=(4,), in_specs=[fix((8, 4096)), fix((8, 16))...  14.1 us
    all_to_all x1, starting transfers between devices, body(): arrived = exchange(sending)  11.7 us
  transfers between devices with their start and end apart: 7, of which 2 were waited for; matrix products, arithmetic and copies ran while one was open for 4% of the time, Pallas kernels for 15%

profile of v5, /device:TPU:1, one launch (start us, length us, event | category | flops | bytes accessed | tf_op | source)
XLA Modules:
  0.0 284.0 jit_solution(1851279823251676091)
XLA Ops:
  0.6 22.2 %k1.1 = bf16[1024,512]{1,0:T(8,128)(2,1)} custom-call(bf16[8,16384]{1,0:T(8,128)(2,1)} %ll_ref.1, s32[128,512]{1,0:T(8,128)} %bitcast.44), custom_call_target="tpu_custom_call" | custom-call | tf_op jit(solution)/shard_map/k1/pallas_call | solution.py:54
  22.9 11.5 %all-to-all-start = ((bf16[128,8,512]{2,1,0:T(8,128)(2,1)}), bf16[128,8,512]{2,1,0:T(8,128)(2,1)S(1)}, u32[]{:S(2)}, u32[]{:S(2)}) async-start(bf16[128,8,512]{2,1,0:T(8,128)(2,1)} %bitcast.36), calls=%async_computation | async-start | bytes 2097152 | tf_op jit(solution)/shard_map/all_to_all | solution.py:407
  34.4 7.3 %prep.5 = (s32[4,1,4096]{2,1,0:T(1,128)}, s32[128,256]{1,0:T(8,128)}, s32[4,1,256]{2,1,0:T(1,128)}) custom-call(s32[4,4096]{1,0:T(4,128)} %slot_ref.5), custom_call_target="tpu_custom_call" | custom-call | flops 6400000000 | bytes 240000 | tf_op jit(solution)/shard_map/prep/pallas_call | solution.py:248
  41.6 1.3 copy.47
  42.9 11.8 %prep.3 = (s32[7,1,4096]{2,1,0:T(1,128)}, s32[224,256]{1,0:T(8,128)}, s32[7,1,256]{2,1,0:T(1,128)}) custom-call(s32[4,16384]{1,0:T(4,128)} %slot_ref.4), custom_call_target="tpu_custom_call" | custom-call | flops 11200000000 | bytes 420000 | tf_op jit(solution)/shard_map/prep/pallas_call | solution.py:248
  54.7 1.0 copy-done.2
  55.7 8.9 %k2.1.reg_ref = bf16[8,4096]{1,0:T(8,128)(2,1)} custom-call(s32[4,256]{1,0:T(4,128)} %bitcast.49, bf16[1024,512]{1,0:T(8,128)(2,1)} %bitcast.35, f32[4,4096]{1,0:T(4,128)} %w_ref.2, s32[4,1,4096]{2,1,0:T(1,128)} %get-tuple-element.35.pos_ref, s32[128,256]{1,0:T(8,128)} %get-tuple-element.36.code_ref), custom_call_target="tpu_custom_call" | custom-call | tf_op jit(solution)/shard_map/k2/pallas_call | solution.py:377
  64.6 0.9 fusion.1
  65.6 1.3 collective-permute-start
  66.9 0.7 slice_bitcast_fusion.1
  67.9 2.9 %collective-permute-done.1.rc_ref = bf16[8,16]{1,0:T(8,128)(2,1)S(1)} collective-permute-done((bf16[8,16]{1,0:T(8,128)(2,1)S(1)}, bf16[8,16]{1,0:T(8,128)(2,1)S(1)}, u32[]{:S(2)}, u32[]{:S(2)}) %collective-permute-start.1) | collective-permute-done | bytes 288 | tf_op jit(solution)/shard_map/ppermute | solution.py:393
  70.9 2.7 collective-permute-start.2
  73.7 3.1 %collective-permute-start.3 = (bf16[8,258]{1,0:T(8,128)(2,1)S(1)}, bf16[8,258]{1,0:T(8,128)(2,1)S(1)}, u32[]{:S(2)}, u32[]{:S(2)}) collective-permute-start(bf16[8,258]{1,0:T(8,128)(2,1)S(1)} %pad_maximum_fusion.2), channel_id=1, source_target_pairs={{0,112},{1,113},{2,114},{3,115},{4,116},{5,117},{6,118},{7,119},{8... | collective-permute-start | bytes 12392 | tf_op jit(solution)/shard_map/ppermute | solution.py:393
  77.6 0.7 copy.37.uw_ref
  79.0 14.1 %kf.1 = (bf16[1024,512]{1,0:T(8,128)(2,1)}, bf16[72,4096]{1,0:T(8,128)(2,1)}) custom-call(bf16[8,4096]{1,0:T(8,128)(2,1)} %k2.1.reg_ref, bf16[8,16]{1,0:T(8,128)(2,1)} %copy-done.7, bf16[8,16]{1,0:T(8,128)(2,1)} %copy-done.8, bf16[8,258]{1,0:T(8,128)(2,1)} %copy-done.12, bf16[8,258]{1,0:T(8,128)(2,1)} %copy-done.13, s32[9,4096]{1,0:T(8,128)} %n3_ref.1, ...), custom_call_target="tpu_custom_call" | custom-call | tf_op jit(solution)/shard_map/kf/pallas_call | solution.py:122
  93.0 11.7 %all-to-all-start.1 = ((bf16[128,8,512]{2,1,0:T(8,128)(2,1)}), bf16[128,8,512]{2,1,0:T(8,128)(2,1)S(1)}, u32[]{:S(2)}, u32[]{:S(2)}) async-start(bf16[128,8,512]{2,1,0:T(8,128)(2,1)} %bitcast.37), calls=%async_computation.1 | async-start | bytes 2097152 | tf_op jit(solution)/shard_map/all_to_all | solution.py:424
  104.7 14.8 %prep.4 = (s32[9,1,4096]{2,1,0:T(1,128)}, s32[288,256]{1,0:T(8,128)}, s32[9,1,256]{2,1,0:T(1,128)}) custom-call(s32[4,16384]{1,0:T(4,128)} %slot_ref.4), custom_call_target="tpu_custom_call" | custom-call | flops 14400000000 | bytes 540000 | tf_op jit(solution)/shard_map/prep/pallas_call | solution.py:248
  119.5 0.7 copy.31
  120.9 1.8 pad_add_fusion.code_ref
  122.7 1.7 pad_add_fusion.1.pos_ref
  124.4 1.0 copy-done.1
  125.3 71.1 %k4.1 = (bf16[8,16384]{1,0:T(8,128)(2,1)}, bf16[1024,512]{1,0:T(8,128)(2,1)}) custom-call(s32[16,256]{1,0:T(8,128)} %add_bitcast_fusion.gid_ref, bf16[1024,512]{1,0:T(8,128)(2,1)} %bitcast.34, bf16[8,16384]{1,0:T(8,128)(2,1)} %tgt_ref.1, f32[4,16384]{1,0:T(4,128)} %w_ref.3, s32[16,1,4096]{2,1,0:T(1,128)} %pad_add_fusion.1.pos_ref, ...), custom_call_target="tpu_custom_call" | custom-call | tf_op jit(solution)/shard_map/k4/pallas_call | solution.py:353
  196.4 11.4 %all-to-all-start.2 = ((bf16[128,8,512]{2,1,0:T(8,128)(2,1)}), bf16[128,8,512]{2,1,0:T(8,128)(2,1)S(1)}, u32[]{:S(2)}, u32[]{:S(2)}) async-start(bf16[128,8,512]{2,1,0:T(8,128)(2,1)} %bitcast.38), calls=%async_computation.2 | async-start | bytes 2097152 | tf_op jit(solution)/shard_map/all_to_all | solution.py:430
  207.8 0.7 copy.41
  208.5 0.7 copy.40
  209.3 8.5 %kr.1 = (bf16[64,4096]{1,0:T(8,128)(2,1)}, bf16[256,4096]{1,0:T(8,128)(2,1)}, f32[256,4096]{1,0:T(8,128)}, bf16[64,4096]{1,0:T(8,128)(2,1)}) custom-call(bf16[72,4096]{1,0:T(8,128)(2,1)} %get-tuple-element.46.st_ref, bf16[64,72]{1,0:T(8,128)(2,1)} %copy.36.cw_ref, bf16[256,64]{1,0:T(8,128)(2,1)} %copy.37.uw_ref, bf16[64,256]{1,0:T(8,128)(2,1)} %dw_ref.3), custom_call_target="tpu_custom_call" | custom-call | flops 10000000000 | bytes 8000000 | tf_op jit(solution)/shard_map/kr/pallas_call | solution.py:143
  217.8 9.3 %all-to-all-done.2 = bf16[128,8,512]{2,1,0:T(8,128)(2,1)S(1)} async-done(((bf16[128,8,512]{2,1,0:T(8,128)(2,1)}), bf16[128,8,512]{2,1,0:T(8,128)(2,1)S(1)}, u32[]{:S(2)}, u32[]{:S(2)}) %all-to-all-start.2) | async-done | bytes 1048608 | tf_op jit(solution)/shard_map/all_to_all | solution.py:430
  227.1 1.0 copy-done
  228.0 22.0 %kb.1 = f32[384,128]{1,0:T(8,128)} custom-call(bf16[1024,512]{1,0:T(8,128)(2,1)} %bitcast.33, s32[128,512]{1,0:T(8,128)} %bitcast.40, bf16[72,4096]{1,0:T(8,128)(2,1)} %get-tuple-element.46.st_ref, bf16[64,4096]{1,0:T(8,128)(2,1)} %get-tuple-element.47.cb_ref, bf16[256,4096]{1,0:T(8,128)(2,1)} %get-tuple-element.48.act_ref, ...), custom_call_target="tpu_custom_call" | custom-call | tf_op jit(solution)/shard_map/kb/pallas_call | solution.py:203
  250.0 1.0 reshape.43
  251.0 15.4 %all_to_all.44 = f32[128,3,128]{2,1,0:T(4,128)S(1)} all-to-all(f32[128,3,128]{2,1,0:T(4,128)S(1)} %reshape.43), channel_id=1, replica_groups=mesh['cells'=128] {'cells'}, dimensions={0} | all-to-all | bytes 393216 | tf_op jit(solution)/shard_map/all_to_all | solution.py:433
  266.6 15.3 %all_to_all.45 = f32[128,3,128]{2,1,0:T(4,128)S(1)} all-to-all(f32[128,3,128]{2,1,0:T(4,128)S(1)} %broadcast_in_dim.2), channel_id=1, replica_groups=mesh['cells'=128] {'cells'}, dimensions={0} | all-to-all | bytes 393216 | tf_op jit(solution)/shard_map/all_to_all | solution.py:434
  (51 shorter events, 5.0 us)
Async XLA Ops:
  22.9 31.8 %all-to-all-start = ((bf16[128,8,512]{2,1,0:T(8,128)(2,1)}), bf16[128,8,512]{2,1,0:T(8,128)(2,1)S(1)}, u32[]{:S(2)}, u32[]{:S(2)}) async-start(bf16[128,8,512]{2,1,0:T(8,128)(2,1)} %bitcast.36), calls=%async_computation | async-start | bytes 2097152 | tf_op jit(solution)/shard_map/all_to_all | solution.py:407
  42.9 33.9 %copy-start.9 = (bf16[64,72]{1,0:T(8,128)(2,1)S(1)}, bf16[64,72]{1,0:T(8,128)(2,1)}, u32[]{:S(2)}) copy-start(bf16[64,72]{1,0:T(8,128)(2,1)} %param.19) | copy-start | bytes 27652
  42.9 34.7 %copy-start.4 = (bf16[256,64]{0,1:T(8,128)(2,1)S(1)}, bf16[256,64]{0,1:T(8,128)(2,1)}, u32[]{:S(2)}) copy-start(bf16[256,64]{0,1:T(8,128)(2,1)} %param.20) | copy-start | bytes 98308
  54.7 1.0 copy-start.2
  65.6 2.2 collective-permute-start
  67.7 3.0 %collective-permute-start.1 = (bf16[8,16]{1,0:T(8,128)(2,1)S(1)}, bf16[8,16]{1,0:T(8,128)(2,1)S(1)}, u32[]{:S(2)}, u32[]{:S(2)}) collective-permute-start(bf16[8,16]{1,0:T(8,128)(2,1)S(1)} %bitcast.51), channel_id=1, source_target_pairs={{0,127},{1,0},{2,1},{3,2},{4,3},{5,4},{6,5},{7,6},{8,7},{9,8},{10,... | collective-permute-start | bytes 776 | tf_op jit(solution)/shard_map/ppermute | solution.py:393
  67.8 10.6 %copy-start.7 = (bf16[8,16]{1,0:T(8,128)(2,1)}, bf16[8,16]{1,0:T(8,128)(2,1)S(1)}, u32[]{:S(2)}) copy-start(bf16[8,16]{1,0:T(8,128)(2,1)S(1)} %collective-permute-done.lc_ref) | copy-start | bytes 772
  70.8 7.6 %copy-start.8 = (bf16[8,16]{1,0:T(8,128)(2,1)}, bf16[8,16]{1,0:T(8,128)(2,1)S(1)}, u32[]{:S(2)}) copy-start(bf16[8,16]{1,0:T(8,128)(2,1)S(1)} %collective-permute-done.1.rc_ref) | copy-start | bytes 772
  70.9 7.4 %collective-permute-start.2 = (bf16[8,258]{1,0:T(8,128)(2,1)S(1)}, bf16[8,258]{1,0:T(8,128)(2,1)S(1)}, u32[]{:S(2)}, u32[]{:S(2)}) collective-permute-start(bf16[8,258]{1,0:T(8,128)(2,1)S(1)} %pad_maximum_fusion.1), channel_id=1, source_target_pairs={{0,16},{1,17},{2,18},{3,19},{4,20},{5,21},{6,22},{7,23},{8,24},{9,... | collective-permute-start | bytes 12392 | tf_op jit(solution)/shard_map/ppermute | solution.py:393
  73.7 4.7 %collective-permute-start.3 = (bf16[8,258]{1,0:T(8,128)(2,1)S(1)}, bf16[8,258]{1,0:T(8,128)(2,1)S(1)}, u32[]{:S(2)}, u32[]{:S(2)}) collective-permute-start(bf16[8,258]{1,0:T(8,128)(2,1)S(1)} %pad_maximum_fusion.2), channel_id=1, source_target_pairs={{0,112},{1,113},{2,114},{3,115},{4,116},{5,117},{6,118},{7,119},{8... | collective-permute-start | bytes 12392 | tf_op jit(solution)/shard_map/ppermute | solution.py:393
  78.4 0.6 copy-start.12
  78.4 0.6 copy-start.13
  93.0 31.3 %all-to-all-start.1 = ((bf16[128,8,512]{2,1,0:T(8,128)(2,1)}), bf16[128,8,512]{2,1,0:T(8,128)(2,1)S(1)}, u32[]{:S(2)}, u32[]{:S(2)}) async-start(bf16[128,8,512]{2,1,0:T(8,128)(2,1)} %bitcast.37), calls=%async_computation.1 | async-start | bytes 2097152 | tf_op jit(solution)/shard_map/all_to_all | solution.py:424
  104.7 15.6 %copy-start.11 = (s32[7,1,256]{2,1,0:T(1,128)S(1)}, s32[7,1,256]{2,1,0:T(1,128)}, u32[]{:S(2)}) copy-start(s32[7,1,256]{2,1,0:T(1,128)} %get-tuple-element.31) | copy-start | bytes 21508
  104.7 16.2 %copy-start.3 = (s32[224,256]{1,0:T(8,128)S(1)}, s32[224,256]{1,0:T(8,128)}, u32[]{:S(2)}) copy-start(s32[224,256]{1,0:T(8,128)} %get-tuple-element.40) | copy-start | bytes 688132
  104.7 18.0 %copy-start.6 = (s32[7,1,4096]{2,1,0:T(1,128)S(1)}, s32[7,1,4096]{2,1,0:T(1,128)}, u32[]{:S(2)}) copy-start(s32[7,1,4096]{2,1,0:T(1,128)} %get-tuple-element.38) | copy-start | bytes 344068
  119.5 88.3 %copy-start.10 = (bf16[8,64]{1,0:T(8,128)(2,1)S(1)}, bf16[8,64]{1,0:T(8,128)(2,1)}, u32[]{:S(2)}) copy-start(bf16[8,64]{1,0:T(8,128)(2,1)} %hw_ref.1) | copy-start | bytes 3076
  119.5 89.0 %copy-start.5 = (bf16[64,256]{1,0:T(8,128)(2,1)S(1)}, bf16[64,256]{1,0:T(8,128)(2,1)}, u32[]{:S(2)}) copy-start(bf16[64,256]{1,0:T(8,128)(2,1)} %dw_ref.3) | copy-start | bytes 98308
  124.4 1.0 copy-start.1
  196.4 30.6 %all-to-all-start.2 = ((bf16[128,8,512]{2,1,0:T(8,128)(2,1)}), bf16[128,8,512]{2,1,0:T(8,128)(2,1)S(1)}, u32[]{:S(2)}, u32[]{:S(2)}) async-start(bf16[128,8,512]{2,1,0:T(8,128)(2,1)} %bitcast.38), calls=%async_computation.2 | async-start | bytes 2097152 | tf_op jit(solution)/shard_map/all_to_all | solution.py:430
  227.0 1.0 copy-start
